TPU v7x, 128 devices: a whole 4x4x4 slice. The times are simulated.
128 devices in a mesh: row: 16 (over y_lo, x, core), col: 8 (over z, y_hi).
Axes of the slice: x: 4, y: 4 (y_hi: 2, y_lo: 2; y = y_hi * 2 + y_lo), z: 4, core: 2. Of those that a mesh axis runs over, the one named last changes fastest.
Arguments:
- spectra: bfloat16 [32, 4096, 512], P(None, ('row', 'col')), may hold values from -6 to 6
- quality: int32 [4096], P(('row', 'col')), may hold values 0 or 1
- tile_mask: int32 [32, 32], replicated, may hold values 0 or 1
Outputs:
- correlations: bfloat16 [64, 4096, 4096], P(None, 'row', 'col')
All inputs are finite; a program needn't handle non-finite values. No bound on the sum of `quality` on one device may be relied on, other than what follows from the above.
Results may differ from a plain program's by a relative error of at most 0.0066.
Values may be sent and summed in bfloat16 or wider, within the bound.
A program may use at most 192 MiB of HBM per device.

v0:
```python
import math

import jax
import jax.numpy as jnp
from jax import lax
from jax.sharding import PartitionSpec as P

F = 32
LAGS = 64
W = 256
BLK = 128


def broadcast(block, axis, source):
    block = jnp.where(lax.axis_index(axis) == source, block, jnp.zeros_like(block))
    return lax.psum(block, axis)


def whiten(spectra, quality):
    values = spectra.astype(jnp.float32)
    half_width = values.shape[2] // 2
    real_part = values[:, :, :half_width]
    imag_part = values[:, :, half_width:]
    energy = real_part * real_part + imag_part * imag_part
    mean_energy = jnp.mean(energy, axis=0, keepdims=True)
    factor = quality.astype(jnp.float32)[None, :, None] / jnp.sqrt(energy + mean_energy + 1e-06)
    return jnp.concatenate([real_part * factor, imag_part * factor], axis=2).astype(jnp.bfloat16)


def make_basis():
    lag_offset = jnp.arange(LAGS, dtype=jnp.float32) - LAGS / 2
    frequency = jnp.arange(F, dtype=jnp.float32) + 1.0
    angles = 2.0 * math.pi * frequency[None, :] * lag_offset[:, None] / (2.0 * LAGS)
    return jnp.stack([jnp.cos(angles), -jnp.sin(angles)], axis=1).astype(jnp.bfloat16)


def per_device(spectra, quality, tile_mask):
    white = whiten(spectra, quality)
    row_block = lax.all_gather(white, "col", axis=1, tiled=True)
    col_index = lax.axis_index("col")
    row_index = lax.axis_index("row")
    lower_block = broadcast(row_block, "row", 2 * col_index)
    upper_block = broadcast(row_block, "row", 2 * col_index + 1)
    col_block = jnp.concatenate([lower_block, upper_block], axis=1)
    half_width = col_block.shape[2] // 2
    turned = jnp.concatenate([-col_block[:, :, half_width:], col_block[:, :, :half_width]], axis=2)
    both_parts = jnp.concatenate([col_block, turned], axis=1)
    row_count = row_block.shape[1]
    col_count = col_block.shape[1]
    blocks = row_count // BLK
    col_tiles = col_count // BLK
    local_mask = lax.dynamic_slice(
        tile_mask, (row_index * blocks, col_index * col_tiles), (blocks, col_tiles)
    ).astype(jnp.float32)
    lag_basis = make_basis()
    norm_scale = 1.0 / math.sqrt(W * F)

    def fill_block(block_index, result):
        rows_here = lax.dynamic_slice_in_dim(row_block, block_index * BLK, BLK, 1)
        cross_spec = jnp.einsum(
            "fiw,fjw->fij", rows_here, both_parts, preferred_element_type=jnp.float32
        ).astype(jnp.bfloat16)
        cross_spec = cross_spec.reshape(F, BLK, 2, col_count)
        lagged = jnp.einsum(
            "lpf,fipj->lij", lag_basis, cross_spec, preferred_element_type=jnp.float32
        )
        mask_tiles = lax.dynamic_index_in_dim(local_mask, block_index, 0, keepdims=False)
        mask_row = jnp.broadcast_to(mask_tiles[:, None], (col_tiles, BLK)).reshape(col_count)
        tile_piece = (lagged * norm_scale * mask_row[None, None, :]).astype(jnp.bfloat16)
        return lax.dynamic_update_slice_in_dim(result, tile_piece, block_index * BLK, 1)

    initial = jnp.zeros((LAGS, row_count, col_count), jnp.bfloat16)
    return lax.fori_loop(0, blocks, fill_block, initial)


def solution(mesh):
    placed = (P(None, ("row", "col"), None), P(("row", "col")), P())
    return jax.shard_map(
        per_device, mesh=mesh, in_specs=placed, out_specs=P(None, "row", "col"), check_vma=False
    )
```

profile of v0, /device:TPU:27, one launch (start us, length us, event | category | flops | bytes accessed | tf_op | source)
XLA Modules:
  0.0 501.3 jit_solution(6806146459636945385)
XLA Ops:
  6.5 0.0 all-gather.2.cloned.1.call-start
  6.5 0.7 convert_element_type.29
  7.2 1.5 convert_element_type.28
  8.7 0.2 fusion.10
  8.9 0.5 multiply_convert_fusion.1
  9.4 1.1 pad_maximum_fusion
  10.5 0.0 all-gather.2.cloned.1.call-update
  10.5 0.0 all-reduce.3.cloned.1.call-start
  10.5 106.6 %all-gather.2.cloned.1.call-done = bf16[32,256,512]{2,1,0:T(8,128)(2,1)} async-done(((bf16[32,32,512]{2,1,0:T(8,128)(2,1)}), bf16[32,256,512]{2,1,0:T(8,128)(2,1)}) %all-gather.2.cloned.1.call-update) | async-done | bytes 8388624 | tf_op jit(solution)/shard_map/all_gather | solution.py:39
  117.1 9.6 %broadcast_select_fusion = (bf16[32,256,512]{2,1,0:T(8,128)(2,1)}, bf16[32,256,512]{2,1,0:T(8,128)(2,1)}) fusion(bf16[32,256,512]{2,1,0:T(8,128)(2,1)} %all-gather.2.cloned.1.call-done, pred[]{:T(512)S(6)} %eq.7, pred[]{:T(512)S(6)} %eq.6), kind=kLoop, calls=%fused_computation.15 | loop fusion | flops 8388608 | bytes 25165826 | tf_op jit(solution)/shard_map/jit(_where)/select_n | solution.py:15
  126.7 0.0 all-reduce.3.cloned.1.call-update
  126.8 0.8 dynamic-slice_convert_fusion
  127.5 0.1 cosine_convert_fusion
  127.7 193.6 %all-reduce.3.cloned.1.call-done = (bf16[32,256,512]{2,1,0:T(8,128)(2,1)}, bf16[32,256,512]{2,1,0:T(8,128)(2,1)}) async-done(((bf16[32,256,512]{2,1,0:T(8,128)(2,1)}, bf16[32,256,512]{2,1,0:T(8,128)(2,1)}), (bf16[32,256,512]{2,1,0:T(8,128)(2,1)}, bf16[32,256,512]{2,1,0:T(8,128)(2,1)})) %all-reduce.3.cloned.1.call-update) | async-done | bytes 16777232 | tf_op jit(solution)/shard_map/psum | solution.py:16
  321.3 7.7 %constant_dynamic-update-slice_fusion.1 = bf16[32,512,512]{2,1,0:T(8,128)(2,1)} fusion(bf16[32,256,512]{2,1,0:T(8,128)(2,1)} %get-tuple-element.127), kind=kLoop, calls=%fused_computation.28 | loop fusion | bytes 16777216
  328.9 7.7 %constant_dynamic-update-slice_fusion = bf16[32,512,512]{2,1,0:T(8,128)(2,1)} fusion(bf16[32,512,512]{2,1,0:T(8,128)(2,1)} %constant_dynamic-update-slice_fusion.1, bf16[32,256,512]{2,1,0:T(8,128)(2,1)} %get-tuple-element.128), kind=kLoop, calls=%fused_computation.27 | loop fusion | bytes 16777216 | tf_op jit(solution)/shard_map/concatenate | solution.py:44
  336.6 11.3 %slice_negate_fusion = (bf16[32,512,256]{2,1,0:T(8,128)(2,1)}, bf16[32,512,256]{2,1,0:T(8,128)(2,1)}) fusion(bf16[32,512,512]{2,1,0:T(8,128)(2,1)} %constant_dynamic-update-slice_fusion), kind=kLoop, calls=%fused_computation.14 | loop fusion | flops 4194304 | bytes 33554432 | tf_op jit(solution)/shard_map/neg | solution.py:46
  347.9 22.6 %maximum_maximum_fusion = bf16[32,1024,512]{2,1,0:T(8,128)(2,1)} fusion(bf16[32,512,256]{2,1,0:T(8,128)(2,1)} %get-tuple-element.130, bf16[32,512,256]{2,1,0:T(8,128)(2,1)} %get-tuple-element.129, bf16[32,256,512]{2,1,0:T(8,128)(2,1)} %get-tuple-element.128, bf16[32,256,512]{2,1,0:T(8,128)(2,1)} %get-tuple-element.127), kind=kLoop, calls=%fused_computation.13 | loop fusion | flops 134217728 | bytes 67108864 | tf_op jit(solution)/shard_map/concatenate | solution.py:47
  370.5 6.0 %broadcast_in_dim.25.clone = bf16[64,256,512]{2,1,0:T(8,128)(2,1)} broadcast(bf16[]{:T(256)} %constant.67.clone.1), dimensions={} | broadcast | bytes 16777218 | tf_op jit(solution)/shard_map/broadcast_in_dim | solution.py:72
  376.6 117.9 %while.13 = (s32[]{:T(128)}, bf16[64,256,512]{2,1,0:T(8,128)(2,1)}, bf16[32,256,512]{2,1,0:T(8,128)(2,1)}, bf16[32,1024,512]{2,1,0:T(8,128)(2,1)}, bf16[64,2,32]...) while((s32[]{:T(128)}, bf16[64,256,512]{2,1,0:T(8,128)(2,1)}, ...), condition=%wide.region_4.5_spmd, body=%wide.region_3.4_spmd.sunk | while | flops 4844421120 | bytes 96481496 | solution.py:73
  376.6 0.1 broadcast_bitcast_fusion.2
  376.7 19.5 %convolution_convert_fusion.2 = bf16[32,128,1024]{2,1,0:T(8,128)(2,1)} fusion(bf16[32,1024,512]{2,1,0:T(8,128)(2,1)} %get-tuple-element.197, bf16[32,256,512]{2,1,0:T(8,128)(2,1)} %get-tuple-element.196, s32[]{:T(128)S(6)} %select_n.45), kind=kOutput, calls=%fused_computation.4.clone.1 | convolution fusion | flops 4299161600 | bytes 46137348 | tf_op jit(solution)/shard_map/while/body/eval_jaxpr/fiw,fjw->fij/dot_general | solution.py:60
  396.1 14.5 %reshape.122 = bf16[32,128,2,512]{3,2,1,0:T(2,128)(2,1)} reshape(bf16[32,128,1024]{2,1,0:T(8,128)(2,1)} %convolution_convert_fusion.2) | data formatting | bytes 16777216 | tf_op jit(solution)/shard_map/while/body/eval_jaxpr/reshape | solution.py:63
  410.6 13.4 %fusion.23 = bf16[64,128,512]{2,0,1:T(8,128)(2,1)} fusion(f32[512]{0:T(512)S(1)} %broadcast_bitcast_fusion.2, bf16[32,128,2,512]{3,2,1,0:T(2,128)(2,1)} %reshape.122, bf16[64,2,32]{0,2,1:T(8,128)(2,1)S(1)} %get-tuple-element.198), kind=kOutput, calls=%fused_computation.5.clone.1 | convolution fusion | flops 545259520 | bytes 16787456 | tf_op jit(solution)/shard_map/while/body/eval_jaxpr/lpf,fipj->lij/dot_general | solution.py:64
  424.0 11.5 %copy_dynamic-update-slice_fusion.2 = bf16[64,256,512]{2,1,0:T(8,128)(2,1)} fusion(bf16[64,256,512]{2,1,0:T(8,128)(2,1)} %get-tuple-element.185, s32[]{:T(128)S(6)} %select_n.45, bf16[64,128,512]{2,0,1:T(8,128)(2,1)} %fusion.23), kind=kLoop, calls=%fused_computation.2.clone.1 | loop fusion | bytes 16777220 | tf_op jit(solution)/shard_map/while/body/eval_jaxpr/dynamic_update_slice | solution.py:70
  435.5 0.1 broadcast_bitcast_fusion.2
  435.6 19.5 %convolution_convert_fusion.2 = bf16[32,128,1024]{2,1,0:T(8,128)(2,1)} fusion(bf16[32,1024,512]{2,1,0:T(8,128)(2,1)} %get-tuple-element.197, bf16[32,256,512]{2,1,0:T(8,128)(2,1)} %get-tuple-element.196, s32[]{:T(128)S(6)} %select_n.45), kind=kOutput, calls=%fused_computation.4.clone.1 | convolution fusion | flops 4299161600 | bytes 46137348 | tf_op jit(solution)/shard_map/while/body/eval_jaxpr/fiw,fjw->fij/dot_general | solution.py:60
  455.1 14.5 %reshape.122 = bf16[32,128,2,512]{3,2,1,0:T(2,128)(2,1)} reshape(bf16[32,128,1024]{2,1,0:T(8,128)(2,1)} %convolution_convert_fusion.2) | data formatting | bytes 16777216 | tf_op jit(solution)/shard_map/while/body/eval_jaxpr/reshape | solution.py:63
  469.5 13.4 %fusion.23 = bf16[64,128,512]{2,0,1:T(8,128)(2,1)} fusion(f32[512]{0:T(512)S(1)} %broadcast_bitcast_fusion.2, bf16[32,128,2,512]{3,2,1,0:T(2,128)(2,1)} %reshape.122, bf16[64,2,32]{0,2,1:T(8,128)(2,1)S(1)} %get-tuple-element.198), kind=kOutput, calls=%fused_computation.5.clone.1 | convolution fusion | flops 545259520 | bytes 16787456 | tf_op jit(solution)/shard_map/while/body/eval_jaxpr/lpf,fipj->lij/dot_general | solution.py:64
  482.9 11.5 %copy_dynamic-update-slice_fusion.2 = bf16[64,256,512]{2,1,0:T(8,128)(2,1)} fusion(bf16[64,256,512]{2,1,0:T(8,128)(2,1)} %get-tuple-element.185, s32[]{:T(128)S(6)} %select_n.45, bf16[64,128,512]{2,0,1:T(8,128)(2,1)} %fusion.23), kind=kLoop, calls=%fused_computation.2.clone.1 | loop fusion | bytes 16777220 | tf_op jit(solution)/shard_map/while/body/eval_jaxpr/dynamic_update_slice | solution.py:70
  (6 shorter events, 0.0 us)
Async XLA Ops:
  6.5 110.6 %all-gather.2.cloned.1.call-start = ((), (), s32[]{:S(2)}) async-start(), calls=%async_computation | async-start | bytes 9437184 | tf_op jit(solution)/shard_map/all_gather | solution.py:39
  10.5 310.8 %all-reduce.3.cloned.1.call-start = ((), (), s32[]{:S(2)}) async-start(), calls=%async_computation.1 | async-start | bytes 33554432 | tf_op jit(solution)/shard_map/psum | solution.py:16
Sparse Core Ops, SparseCore 0:
  10.6 106.4 all-gather.1
  126.8 194.3 all-reduce.2
where the time goes:
time: 504 us; the launch traced here: 501 us
  waiting for transfers between devices  300 us (60%)
  local copies, waits for them, and re-layouts  73.4 us (15%)
  matrix products  65.7 us (13%)
  other arithmetic  48.3 us (10%)
  between operations  13.5 us (3%)
    psum x1, waiting for transfers between devices, broadcast(): return lax.psum(block, axis)  194 us
    all_gather x1, waiting for transfers between devices, per_device(): row_block = lax.all_gather(white, 'col', axis=1, tiled=True)  107 us
    dot_general x2, matrix products, fill_block(): jnp.einsum('fiw,fjw->fij', rows_here, both_parts, preferred_element_type=...  38.9 us
    reshape x2, local copies, waits for them, and re-layouts, fill_block(): cross_spec = cross_spec.reshape(F, BLK, 2, col_count)  28.9 us
    dot_general x2, matrix products, fill_block(): jnp.einsum('lpf,fipj->lij', lag_basis, cross_spec, preferred_element_type...  26.8 us
    dynamic_update_slice x2, local copies, waits for them, and re-layouts, fill_block(): lax.dynamic_update_slice_in_dim(result, tile_piece, block_index * BLK, 1)  23 us
    concatenate x1, other arithmetic, per_device(): both_parts = jnp.concatenate([col_block, turned], axis=1)  22.6 us
    neg x1, other arithmetic, per_device(): -col_block[:, :, half_width:]  11.3 us
  transfers between devices with their start and end apart: 2, of which 2 were waited for; matrix products, arithmetic and copies ran while one was open for 0% of the time, Pallas kernels for 0%

commit v1 on v0

v1 whole, which is shorter than its diff:
```python
import functools
import math

import jax
import jax.numpy as jnp
import numpy as np
from jax import lax
from jax.experimental import pallas as pl
from jax.experimental.pallas import tpu as pltpu
from jax.sharding import PartitionSpec as P

F = 32
LAGS = 64
HALF = LAGS // 2
W = 256
BLK = 128
CH = 32
NC = 8
NF = F // NC
MESH = pl.DeviceIdType.MESH

ROW = {'E1': (2, 4), 'E3': (2, 4), 'P0': (4, 12), 'P1': (11, 9), 'E2': (11, 6), 'P3': (15, 8), 'P2': (15, 7)}
NAMES = {'E0': 'a0', 'P0': 'a1', 'P1': 'a2', 'E1': 'b0', 'E3': 'b1', 'E2': 'b2', 'P3': 'y0', 'P2': 'y1'}
PIECE = {n: p for p, n in NAMES.items()}
COL = {'a0': (5, ((0, 2, 4, 5), (8, 6, 9, 10))), 'a1': (9, ((6, 11, 12, 13), (22, 19, 15, 18))),
       'a2': (6, ((13, 17, 18, 19), (21, 18, 20, 23))), 'b0': (8, ((0, 8, 7, 6), (9, 11, 10, 7))),
       'b1': (10, ((0, 6, 5, 4), (13, 12, 10, 12))), 'b2': (4, ((14, 23, 22, 21), (26, 29, 26, 22))),
       'y0': (6, ((17, 9, 11, 9), (5, 7, 8, 7))), 'y1': (6, ((17, 21, 23, 21), (17, 19, 22, 19)))}
MUL = (29, 5)
ENTRY = {0: ('y0', 'y1'), 1: ('a0', 'a2'), 2: ('a1', 'b1'), 3: ('b0', 'b2')}
TICKS = MUL[0] + (MUL[1] * (NC - 1)) // 4 + 1


def whiten(spectra, quality):
    values = spectra.astype(jnp.float32)
    half_width = values.shape[2] // 2
    real_part = values[:, :, :half_width]
    imag_part = values[:, :, half_width:]
    energy = real_part * real_part + imag_part * imag_part
    mean_energy = jnp.mean(energy, axis=0, keepdims=True)
    factor = quality.astype(jnp.float32)[None, :, None] / jnp.sqrt(energy + mean_energy + 1e-06)
    return jnp.concatenate([real_part * factor, imag_part * factor], axis=2).astype(jnp.bfloat16)


def any_of(q, places):
    hit = q < 0
    for place in places:
        hit = hit | (q == place)
    return hit


def pick(mirror, q, table):
    value = jnp.int32(table[0][0])
    for m in range(2):
        for place in range(4):
            value = jnp.where((mirror == m) & (q == place), table[m][place], value)
    return value


def gather_kernel(white, cross, rowb, colb, passb, local_sem, row_sem, row2_sem, pass_sem, col_sem, sib_sem,
                  srow_sem, sy_sem, sr_sem, scol_sem):
    row, col = lax.axis_index("row"), lax.axis_index("col")
    core, x, y_lo = row % 2, (row // 2) % 4, row // 8
    z, y_hi = col // 2, col % 2
    y = y_hi * 2 + y_lo

    def at(xx, yy, zz, cc):
        return {"row": (yy % 2) * 8 + xx * 2 + cc, "col": zz * 2 + yy // 2}

    x_up, x_dn = at((x + 1) % 4, y, z, core), at((x + 3) % 4, y, z, core)
    y_up, y_dn = at(x, (y + 1) % 4, z, core), at(x, (y + 3) % 4, z, core)
    z_up, z_dn = at(x, y, (z + 1) % 4, core), at(x, y, (z + 3) % 4, core)
    sibling = at(x, y, z, 1 - core)
    pair = at(x, y_hi * 2 + 1 - y_lo, z, core)
    other = at(x, (y + 3 + 2 * y_lo) % 4, z, core)

    q = (x + 4 - col % 4) % 4
    mirror = (y_lo + 2 - col // 4) % 2
    k = y_lo * 4 + x
    is_root = k == col
    feeds = (z == k // 2) & (y_hi != k % 2)

    def ident(piece):
        half = y_hi if piece[0] == 'E' else 1 - y_hi
        return ((z + int(piece[1])) % 4) * 2 + half

    ids = {p: ident(p) for p in NAMES}

    def chunk(g):
        return pl.ds(g * NF, NF)

    def remote(src, dst, send, recv, to):
        pltpu.make_async_remote_copy(src, dst, send, recv, device_id=to, device_id_type=MESH).start()

    def row_send(slot, piece, g, to):
        part = rowb.at[ids[piece], chunk(g)]
        remote(part, part, srow_sem.at[slot], row_sem.at[ids[piece], g], to)

    def col_send(src, slot, way, piece, g, to):
        dst = colb.at[core * 8 + ids[piece], chunk(g)]
        remote(dst if src is None else src, dst, scol_sem.at[slot, way], col_sem.at[ids[piece], g], to)

    def sib_send(src, slot, piece, g):
        dst = colb.at[core * 8 + ids[piece], chunk(g)]
        remote(dst if src is None else src, dst, scol_sem.at[slot, 3], sib_sem.at[ids[piece], g], sibling)

    def done(ref, sem):
        pltpu.make_async_copy(ref, ref, sem).wait()

    slots = {n: i for i, n in enumerate(PIECE)}
    own = pltpu.make_async_copy(white, rowb.at[ids['E0']], local_sem)
    own.start()
    barrier = pltpu.get_barrier_semaphore()
    for peer in (x_up, x_dn, y_up, y_dn, z_up, z_dn, sibling):
        pl.semaphore_signal(barrier, inc=1, device_id=peer, device_id_type=MESH)
    pl.semaphore_wait(barrier, 7)
    own.wait()

    def root_step(piece, g):
        name = NAMES[piece]
        src = rowb.at[ids[piece], chunk(g)]
        if name[0] == 'a':
            col_send(src, slots[name], 0, piece, g, x_up)
        if name[0] == 'b':
            col_send(src, slots[name], 1, piece, g, x_dn)
        sib_send(src, slots[name], piece, g)
        pltpu.make_async_copy(src, colb.at[core * 8 + ids[piece], chunk(g)], col_sem.at[ids[piece], g]).start()

    def first(g, carry):
        row_send(0, 'E0', g, z_up)
        row_send(1, 'E0', g, z_dn)

        @pl.when(is_root)
        def _():
            root_step('E0', g)

        return carry

    lax.fori_loop(0, NC, first, 0)

    hf = NF // 2

    def y_own(g):
        src = rowb.at[ids['E0'], pl.ds(g * NF, hf)]
        remote(src, passb.at[0, g], sy_sem.at[0], pass_sem.at[0, g], y_up)
        src = rowb.at[ids['E0'], pl.ds(g * NF + hf, hf)]
        remote(src, passb.at[1, g], sy_sem.at[1], pass_sem.at[1, g], y_dn)

    low_id = z * 2 + (y + 3) % 4 // 2
    high_id = z * 2 + (y + 1) % 4 // 2

    def y_pass(g):
        done(passb.at[0, g], pass_sem.at[0, g])
        remote(passb.at[0, g], rowb.at[low_id, pl.ds(g * NF, hf)], sy_sem.at[2], row_sem.at[low_id, g], y_up)
        done(passb.at[1, g], pass_sem.at[1, g])
        remote(passb.at[1, g], rowb.at[high_id, pl.ds(g * NF + hf, hf)], sy_sem.at[3], row2_sem.at[g], y_dn)

    def row_step(piece, g):
        if piece == 'P0':
            done(rowb.at[ids[piece], pl.ds(g * NF, hf)], row_sem.at[ids[piece], g])
            done(rowb.at[ids[piece], pl.ds(g * NF + hf, hf)], row2_sem.at[g])
        else:
            done(rowb.at[ids[piece], chunk(g)], row_sem.at[ids[piece], g])
        if piece == 'E3':
            row_send(2, piece, g, z_up)
        if piece == 'P0':
            row_send(3, piece, g, z_up)
            row_send(4, piece, g, z_dn)
        if piece == 'P1':
            row_send(5, piece, g, z_dn)

        @pl.when(is_root)
        def _():
            root_step(piece, g)

        if piece in ('E3', 'E2'):
            @pl.when(feeds)
            def _():
                dst = colb.at[core * 8 + ids[piece], chunk(g)]
                remote(rowb.at[ids[piece], chunk(g)], dst, sr_sem.at[0 if piece == 'E3' else 1],
                       col_sem.at[ids[piece], g], other)

    on_root_row = mirror == 0
    ways = {}
    for name in slots:
        up = on_root_row & any_of(q, (1, 2)) & (name[0] == 'a')
        down = on_root_row & any_of(q, (3, 2)) & (name[0] == 'b')
        over = jnp.where(on_root_row, any_of(q, [p for p in (1, 2, 3) if name in ENTRY[p]]),
                         any_of(q, (1, 2, 3)) & (name[0] == 'y'))
        enters = [p for p in range(4) if name in ENTRY[p]][0]
        order = ENTRY[enters].index(name)
        mirrored = mirror == 1
        full = mirrored & (q == enters)
        up_half = mirrored & (q == (enters + 1) % 4)
        down_half = mirrored & (q == (enters + 3) % 4)
        ways[name] = (up | full, up_half, down | full, down_half, over, order)

    def col_step(name, g):
        piece = PIECE[name]
        slot = slots[name]
        done(colb.at[core * 8 + ids[piece], chunk(g)], col_sem.at[ids[piece], g])
        up, up_half, down, down_half, over, order = ways[name]

        @pl.when(up | (up_half & (g % 2 == order)))
        def _():
            col_send(None, slot, 0, piece, g, x_up)

        @pl.when(down | (down_half & (g % 2 != order)))
        def _():
            col_send(None, slot, 1, piece, g, x_dn)

        @pl.when(over)
        def _():
            col_send(None, slot, 2, piece, g, pair)

        sib_send(None, slot, piece, g)

    def multiply(g):
        @pl.when(is_root)
        def _():
            for p in NAMES:
                done(colb.at[core * 8 + ids[p], chunk(g)], col_sem.at[ids[p], g])

        for p in NAMES:
            done(colb.at[(1 - core) * 8 + ids[p], chunk(g)], sib_sem.at[ids[p], g])

        def two_bins(h, carry):
            parts = []
            for e in range(2):
                f = g * NF + h * 2 + e
                lhs = rowb[:, f].reshape(8 * CH, 2 * W)
                turned = jnp.concatenate([lhs[:, W:], -lhs[:, :W]], axis=1)
                rhs = colb[:, f].reshape(16 * CH, 2 * W)
                parts.append(lax.dot_general(jnp.concatenate([lhs, turned], axis=0), rhs, (((1,), (1,)), ((), ())),
                                             preferred_element_type=jnp.float32))
            for c in range(2):
                both = [p[c * 256:(c + 1) * 256].reshape(32, 8, 512) for p in parts]
                cross[c, :, g * (NF // 2) + h] = jnp.concatenate(both, axis=1).astype(jnp.bfloat16)
            return carry

        lax.fori_loop(0, NF // 2, two_bins, 0)

    not_root = jnp.logical_not(is_root)
    always = row >= 0
    jobs = [(y_own, 0, 8, always), (y_pass, 2, 8, always)]
    for piece in ('E3', 'E1', 'P0', 'P1', 'E2', 'P3', 'P2'):
        jobs.append((functools.partial(row_step, piece), *ROW[piece], always))
    for name in ('a0', 'b0', 'y0', 'b1', 'a1', 'y1', 'a2', 'b2'):
        rate, table = COL[name]
        jobs.append((functools.partial(col_step, name), pick(mirror, q, table), rate, not_root))
    jobs.append((multiply, *MUL, always))

    def tick(t, state):
        after = []
        for (act, start, rate, on), g in zip(jobs, state):
            due = on & (g < NC) & (t >= start + (rate * g) // 4)

            @pl.when(due)
            def _(act=act, g=g):
                act(g)

            after.append(g + due.astype(jnp.int32))
        return tuple(after)

    lax.fori_loop(0, TICKS, tick, tuple(jnp.int32(0) for _ in jobs))

    whole = rowb.at[0]
    half_piece = rowb.at[0, pl.ds(0, F // 2)]
    for i in range(6):
        done(whole, srow_sem.at[i])
    for i in range(4):
        done(half_piece, sy_sem.at[i])

    @pl.when(feeds)
    def _():
        done(whole, sr_sem.at[0])
        done(whole, sr_sem.at[1])

    for name in slots:
        up, up_half, down, down_half, over, _ = ways[name]
        slot = slots[name]
        for way, full, part, letter in ((0, up, up_half, 'a'), (1, down, down_half, 'b')):
            @pl.when(jnp.where(is_root, name[0] == letter, full))
            def _(slot=slot, way=way):
                done(whole, scol_sem.at[slot, way])

            @pl.when(not_root & part)
            def _(slot=slot, way=way):
                done(half_piece, scol_sem.at[slot, way])

        @pl.when(not_root & over)
        def _(slot=slot):
            done(whole, scol_sem.at[slot, 2])

        done(whole, scol_sem.at[slot, 3])


def gather_cross(white):
    piece = (F, CH, 2 * W)
    return pl.pallas_call(
        gather_kernel,
        out_shape=pltpu.VMEM((2, 32, F // 2, 16, 512), jnp.bfloat16),
        in_specs=[pl.BlockSpec(memory_space=pltpu.VMEM)],
        out_specs=pl.BlockSpec(memory_space=pltpu.VMEM),
        scratch_shapes=[
            pltpu.VMEM((8, *piece), jnp.bfloat16),
            pltpu.VMEM((16, *piece), jnp.bfloat16),
            pltpu.VMEM((2, NC, NF // 2, CH, 2 * W), jnp.bfloat16),
            pltpu.SemaphoreType.DMA,
            pltpu.SemaphoreType.DMA((8, NC)),
            pltpu.SemaphoreType.DMA((NC,)),
            pltpu.SemaphoreType.DMA((2, NC)),
            pltpu.SemaphoreType.DMA((8, NC)),
            pltpu.SemaphoreType.DMA((8, NC)),
            pltpu.SemaphoreType.DMA((6,)),
            pltpu.SemaphoreType.DMA((4,)),
            pltpu.SemaphoreType.DMA((2,)),
            pltpu.SemaphoreType.DMA((8, 4)),
        ],
        compiler_params=pltpu.CompilerParams(collective_id=0, has_side_effects=True, vmem_limit_bytes=40 << 20),
        name="gather_cross",
    )(white)


def lag_matrices():
    lag = np.arange(HALF + 1, dtype=np.float32)
    frequency = np.arange(F, dtype=np.float32) + np.float32(1.0)
    angles = np.float32(2.0 * math.pi) * frequency[None, :] * lag[:, None] / np.float32(2.0 * LAGS)
    eye = np.eye(8, dtype=np.float32)
    return [np.kron(m, eye).astype(jnp.bfloat16) for m in (np.cos(angles), -np.sin(angles))]


def lag_kernel(mask, cross, even_mat, odd_mat, out):
    cols = out.shape[2]
    step = pl.program_id(0)
    tile_row = lax.axis_index("row") * 2 + step // 8
    tile_col = lax.axis_index("col") * (cols // BLK)
    scale = jnp.concatenate(
        [jnp.full((1, BLK), mask[tile_row, tile_col + t].astype(jnp.float32) * (1.0 / math.sqrt(W * F)), jnp.float32)
         for t in range(cols // BLK)], axis=1)
    even, odd = [], []
    for h in range(2):
        at = step * 2 + h
        even.append(jnp.dot(even_mat[...], cross[0, at].reshape(F * 8, cols), preferred_element_type=jnp.float32))
        odd.append(jnp.dot(odd_mat[...], cross[1, at].reshape(F * 8, cols), preferred_element_type=jnp.float32))
    for m in range(HALF + 1):
        e = [v[m * 8:m * 8 + 8] for v in even]
        o = [v[m * 8:m * 8 + 8] for v in odd]
        if m < HALF:
            out[HALF + m] = (jnp.concatenate([a + b for a, b in zip(e, o)], 0) * scale).astype(out.dtype)
        if m > 0:
            out[HALF - m] = (jnp.concatenate([a - b for a, b in zip(e, o)], 0) * scale).astype(out.dtype)


def lag_transform(cross, tile_mask):
    rows, cols = 256, 512
    even_mat, odd_mat = lag_matrices()
    return pl.pallas_call(
        lag_kernel,
        grid=(rows // 16,),
        in_specs=[
            pl.BlockSpec(memory_space=pltpu.SMEM),
            pl.BlockSpec(memory_space=pltpu.VMEM),
            pl.BlockSpec(even_mat.shape, lambda i: (0, 0)),
            pl.BlockSpec(odd_mat.shape, lambda i: (0, 0)),
        ],
        out_specs=pl.BlockSpec((LAGS, 16, cols), lambda i: (0, i, 0)),
        out_shape=jax.ShapeDtypeStruct((LAGS, rows, cols), jnp.bfloat16),
        compiler_params=pltpu.CompilerParams(vmem_limit_bytes=30 << 20),
        name="lag_transform",
    )(tile_mask, cross, even_mat, odd_mat)


def per_device(spectra, quality, tile_mask):
    cross = gather_cross(whiten(spectra, quality))
    return lag_transform(cross, tile_mask)


def solution(mesh):
    placed = (P(None, ("row", "col"), None), P(("row", "col")), P())
    return jax.shard_map(
        per_device, mesh=mesh, in_specs=placed, out_specs=P(None, "row", "col"), check_vma=False
    )
```

time: 504 us -> 159 us (0.32)
  waiting for transfers between devices: 300 us -> 0 us
  Pallas kernels: 0 us -> 152 us
  local copies, waits for them, and re-layouts: 73.4 us -> 0.01 us
  matrix products: 65.7 us -> 0 us
  other arithmetic: 48.3 us -> 3.89 us
  between operations: 13.5 us -> 0.06 us
    psum x1 -> x0, waiting for transfers between devices: 194 us -> none  [broadcast(): return lax.psum(block, axis)]
    pallas_call x0 -> x2, Pallas kernels: none -> 152 us  [the longest x1 139 us: gather_cross(): pl.pallas_call(gather_kernel, out_shape=pltpu.VMEM((2, 32, F // 2, 16, 51...]
    all_gather x1 -> x0, waiting for transfers between devices: 107 us -> none  [per_device(): row_block = lax.all_gather(white, 'col', axis=1, tiled=True)]
    dot_general x4 -> x0, matrix products: 65.7 us -> none  [the longest x2 38.9 us: fill_block(): jnp.einsum('fiw,fjw->fij', rows_here, both_parts, preferred_element_type=...]
    reshape x2 -> x0, local copies, waits for them, and re-layouts: 28.9 us -> none  [fill_block(): cross_spec = cross_spec.reshape(F, BLK, 2, col_count)]
    dynamic_update_slice x2 -> x0, local copies, waits for them, and re-layouts: 23 us -> none  [fill_block(): lax.dynamic_update_slice_in_dim(result, tile_piece, block_index * BLK, 1)]
    concatenate x1 -> x0, other arithmetic: 22.6 us -> none  [per_device(): both_parts = jnp.concatenate([col_block, turned], axis=1)]
    neg x1 -> x0, other arithmetic: 11.3 us -> none  [per_device(): -col_block[:, :, half_width:]]
  transfers between devices with their start and end apart: 2 -> 0, of which waited for: 2 -> 0; matrix products, arithmetic and copies ran while one was open for 0% -> 0% of each run, Pallas kernels for 0% -> 0%
where the time goes in v1:
time: 159 us; the launch traced here: 156 us
  Pallas kernels  152 us (96%)
  other arithmetic  3.89 us (2%)
    pallas_call x1, Pallas kernels, gather_cross(): pl.pallas_call(gather_kernel, out_shape=pltpu.VMEM((2, 32, F // 2, 16, 51...  139 us
    pallas_call x1, Pallas kernels, lag_transform(): pl.pallas_call(lag_kernel, grid=(rows // 16,), in_specs=[pl.BlockSpec(mem...  13 us

profile of v1, /device:TPU:27, one launch (start us, length us, event | category | flops | bytes accessed | tf_op | source)
XLA Modules:
  0.0 156.2 jit_solution(3561154395381112636)
XLA Ops:
  0.0 0.7 convert_element_type.8
  0.7 1.5 convert_element_type.7
  2.2 0.2 fusion
  2.3 0.5 multiply_convert_fusion.1
  2.9 1.1 pad_maximum_fusion.white
  3.9 0.0 copy-start
  3.9 0.0 copy-start.1
  3.9 0.0 copy-start.2
  3.9 139.2 %gather_cross.1.cross = bf16[2,32,16,16,512]{4,3,2,1,0:T(8,128)(2,1)S(1)} custom-call(bf16[32,32,512]{2,1,0:T(8,128)(2,1)} %pad_maximum_fusion.white), custom_call_target="tpu_custom_call" | custom-call | tf_op jit(solution)/shard_map/gather_cross/pallas_call | solution.py:300
  143.1 0.0 copy-done
  143.1 0.0 copy-done.1
  143.2 0.0 copy-done.2
  143.2 13.0 %lag_transform.1 = bf16[64,256,512]{2,1,0:T(8,128)(2,1)} custom-call(s32[32,32]{1,0:T(8,128)S(1)} %copy-done.2, bf16[2,32,16,16,512]{4,3,2,1,0:T(8,128)(2,1)S(1)} %gather_cross.1.cross, bf16[264,256]{1,0:T(8,128)(2,1)S(1)} %copy-done.1, bf16[264,256]{1,0:T(8,128)(2,1)S(1)} %copy-done), custom_call_target="tpu_custom_call" | custom-call | tf_op jit(solution)/shard_map/lag_transform/pallas_call | solution.py:358
  (1 shorter events, 0.0 us)
Async XLA Ops:
  3.9 139.2 %copy-start = (bf16[264,256]{1,0:T(8,128)(2,1)S(1)}, bf16[264,256]{1,0:T(8,128)(2,1)}, u32[]{:S(2)}) copy-start(bf16[264,256]{1,0:T(8,128)(2,1)} %constant.12.clone.odd_mat) | copy-start | bytes 405508
  3.9 139.2 %copy-start.1 = (bf16[264,256]{1,0:T(8,128)(2,1)S(1)}, bf16[264,256]{1,0:T(8,128)(2,1)}, u32[]{:S(2)}) copy-start(bf16[264,256]{1,0:T(8,128)(2,1)} %constant.11.clone.even_mat) | copy-start | bytes 405508
  3.9 139.2 %copy-start.2 = (s32[32,32]{1,0:T(8,128)S(1)}, s32[32,32]{1,0:T(8,128)}, u32[]{:S(2)}) copy-start(s32[32,32]{1,0:T(8,128)} %mask.1) | copy-start | bytes 12292

commit v2 on v1

--- a/solution.py
+++ b/solution.py
@@ -15,20 +15,74 @@
 W = 256
 BLK = 128
 CH = 32
+MESH = pl.DeviceIdType.MESH
+
+NAMES = {'E1': 'a0', 'P0': 'a1', 'E2': 'a2', 'E0': 'b0', 'E3': 'b1', 'P3': 'b2', 'P1': 'y0', 'P2': 'y1'}
+ENTRY = {0: ('y0', 'y1'), 1: ('a0', 'a2'), 2: ('b1', 'a1'), 3: ('b0', 'b2')}
 NC = 8
+BEFORE, BETWEEN = 37, 5
+ORDER = (
+    (8389120, 8675344, 12846097, 795682, 9446947, 13109268, 1321509, 10234918, 1598999, 1867856, 13664864, 25461841,
+     21523011, 134217328, 134217727, 134217727, 134217727, 134217727, 134217727, 134217727, 134217727, 134217727,
+     134217727, 134217727, 134217727, 134217727, 134217727, 134217727, 134217727, 134217727, 134217727, 134217727,
+     134217727, 134217727, 134217727, 134217727, 134217727, 29657171, 134217727, 134217727, 134217727, 134217727,
+     22070326, 134014007, 134217727, 134217727, 134217727, 22579797, 26011206, 134217727, 134217727, 134217727,
+     18656868, 134217332, 134217727, 134217727, 134217727, 134015589, 134217727, 134217727, 134217727, 134217727,
+     134016102, 134217727, 134217727, 134217727, 134217727, 134016615, 134217727, 134217727, 134217727, 134217727),
+    (4194816, 4481056, 12846113, 8922240, 812176, 46155283, 9447553, 13371569, 9710225, 58786994, 9972741, 6096563,
+     47212583, 59049990, 47480912, 1862290, 34958401, 21283042, 35221058, 17613366, 14487232, 38634066, 50913507,
+     21874848, 38897220, 22070501, 42305649, 51700966, 22400661, 26035398, 30181974, 42852551, 54585431, 134217727,
+     134217727, 134217727, 134217727, 18401430, 134062833, 134217727, 134217727, 134217727, 18664100, 39691381,
+     134217458, 134217727, 134217727, 43314278, 31248115, 55437478, 134217727, 134217727, 134064295, 134217727,
+     134217727, 134217727, 134217727, 134064885, 134217727, 134217727, 134217727, 134217727, 134065398, 134217727,
+     134217727, 134217727, 134217727, 134065911, 134217727, 134217727, 134217727, 134217727),
+    (4194816, 4481056, 12846113, 8922288, 4982449, 46727203, 37767188, 46949380, 33835541, 5769908, 47522342,
+     13389335, 47713410, 58753104, 1928835, 13699137, 25264353, 38306897, 17613505, 59271813, 29402306, 21857926,
+     59575921, 38578372, 51759158, 29919330, 51932832, 60089941, 22646420, 54608614, 39118917, 26059495, 42503255,
+     134078674, 134217727, 134217727, 134217727, 26560100, 39381575, 55372902, 31248036, 134217457, 55914196,
+     43625637, 134217458, 134217727, 134217727, 63786711, 134217727, 134217727, 134217727, 134217727, 134217460,
+     134217727, 134217727, 134217727, 134217727, 134217461, 134217727, 134217727, 134217727, 134217727, 134081783,
+     134217727, 134217727, 134217727, 134217727, 134217727, 134217727, 134217727, 134217727, 134217727),
+    (46137856, 12591136, 4473521, 46686722, 13116450, 9266691, 9529363, 13371412, 9792128, 1425429, 10054800,
+     48038422, 13643303, 38126086, 16818368, 34082357, 59278017, 21282947, 14189762, 51167876, 21570627, 14452932,
+     51710691, 35244144, 51947106, 35506757, 29724244, 26027750, 60613840, 54831776, 18394260, 63022195, 134217727,
+     134217727, 134217727, 134217727, 134217727, 39095969, 30453348, 134217457, 134217727, 134217727, 26559699,
+     63547509, 134217727, 134217727, 134217727, 42789990, 31248085, 63810710, 134217727, 134217727, 64073380,
+     134217727, 134217727, 134217727, 134217727, 64309911, 134217727, 134217727, 134217727, 134217727, 64573094,
+     134217727, 134217727, 134217727, 134217727, 134217463, 134217727, 134217727, 134217727, 134217727),
+    (4194816, 8659488, 12846128, 58737682, 9184771, 9447649, 13109424, 46418453, 1376482, 13388822, 46681623,
+     33932806, 59801680, 17088519, 60104883, 47219793, 25494580, 60360259, 60648018, 38068356, 29657171, 62941878,
+     48015458, 29912197, 63245504, 14453333, 18394258, 35513459, 63800419, 22857921, 54585415, 134037748, 134217727,
+     134217727, 134217727, 134217727, 134217727, 54848101, 134038261, 134217727, 134217727, 134217727, 51440742,
+     27084022, 134063223, 134217727, 134217727, 38635255, 134063779, 134217727, 134217727, 134217727, 43100357,
+     55921350, 52276390, 56446613, 134217364, 134217727, 134217727, 134217727, 134217727, 134217727, 134217366,
+     134217727, 134217727, 134217727, 134217727, 134217367, 134217727, 134217727, 134217727, 134217727),
+    (8389120, 4473360, 12846128, 795682, 33564195, 5261362, 13371616, 58993189, 9964161, 46489622, 6049332, 37752034,
+     16818306, 1862322, 34457153, 17343072, 25544849, 46991427, 21523685, 29388468, 34983104, 47482963, 25758951,
+     38330964, 29953718, 42066113, 42304597, 18132067, 48095859, 42526807, 18401475, 51463922, 30707301, 26814195,
+     51767414, 31248036, 134062289, 134217727, 134217727, 134217727, 134217727, 134217727, 51989237, 38882550,
+     52252407, 55158421, 134217727, 134217727, 134217727, 134217727, 134217727, 134217727, 39692950, 134217428,
+     134217727, 134217727, 134217727, 134217727, 134217727, 134217727, 134217727, 134217727, 134217430, 134217727,
+     134217727, 134217727, 134217727, 134217431, 134217727, 134217727, 134217727, 134217727),
+    (8389120, 8675344, 12846097, 795682, 4998706, 46147620, 9725444, 33645077, 10035205, 59097110, 6049332, 46727686,
+     59277392, 17113607, 34170421, 17343072, 25455796, 34457155, 21594167, 59861616, 29664914, 50687108, 50973268,
+     29919330, 51212006, 34924117, 22644967, 18163334, 35512436, 22857413, 42049606, 134217727, 134217727, 134217727,
+     134217727, 134217727, 134217727, 54839494, 26552481, 63236679, 134217727, 134217727, 26840786, 63521910,
+     134217727, 134217727, 134217727, 31248021, 55389347, 134217459, 134217727, 134217727, 43069172, 134217428,
+     134217727, 134217727, 134217727, 55921397, 134217727, 134217727, 134217727, 134217727, 64875686, 134217430,
+     134217727, 134217727, 134217727, 134065831, 134217727, 134217727, 134217727, 134217727),
+    (4194816, 8659488, 12846128, 46154770, 9184771, 9447601, 13109472, 59001365, 5769906, 6055462, 33670183,
+     21063174, 47259712, 59539975, 21282868, 47514178, 17613457, 47776996, 60065874, 34398261, 25788599, 60328531,
+     22094902, 14536305, 29935236, 22381296, 54625413, 30182486, 54888177, 55150663, 30453348, 26545394, 38604405,
+     63761510, 27101907, 55699575, 134037702, 134038229, 134217727, 134217727, 134217727, 134217727, 56174837,
+     56463094, 134217378, 134217727, 134217727, 42856085, 134217727, 134217727, 134217727, 134217727, 134217380,
+     134217727, 134217727, 134217727, 134217727, 39668886, 134217381, 134217727, 134217727, 134217727, 134217727,
+     134217727, 134217727, 134217727, 134217727, 134217383, 134217727, 134217727, 134217727, 134217727),
+)
 NF = F // NC
-MESH = pl.DeviceIdType.MESH
-
-ROW = {'E1': (2, 4), 'E3': (2, 4), 'P0': (4, 12), 'P1': (11, 9), 'E2': (11, 6), 'P3': (15, 8), 'P2': (15, 7)}
-NAMES = {'E0': 'a0', 'P0': 'a1', 'P1': 'a2', 'E1': 'b0', 'E3': 'b1', 'E2': 'b2', 'P3': 'y0', 'P2': 'y1'}
+ROWS = ('E3', 'E1', 'P0', 'P1', 'E2', 'P3', 'P2')
+ITEMS = ('own', *ROWS, *sorted(NAMES.values()))
 PIECE = {n: p for p, n in NAMES.items()}
-COL = {'a0': (5, ((0, 2, 4, 5), (8, 6, 9, 10))), 'a1': (9, ((6, 11, 12, 13), (22, 19, 15, 18))),
-       'a2': (6, ((13, 17, 18, 19), (21, 18, 20, 23))), 'b0': (8, ((0, 8, 7, 6), (9, 11, 10, 7))),
-       'b1': (10, ((0, 6, 5, 4), (13, 12, 10, 12))), 'b2': (4, ((14, 23, 22, 21), (26, 29, 26, 22))),
-       'y0': (6, ((17, 9, 11, 9), (5, 7, 8, 7))), 'y1': (6, ((17, 21, 23, 21), (17, 19, 22, 19)))}
-MUL = (29, 5)
-ENTRY = {0: ('y0', 'y1'), 1: ('a0', 'a2'), 2: ('a1', 'b1'), 3: ('b0', 'b2')}
-TICKS = MUL[0] + (MUL[1] * (NC - 1)) // 4 + 1
 
 
 def whiten(spectra, quality):
@@ -49,16 +103,7 @@
     return hit
 
 
-def pick(mirror, q, table):
-    value = jnp.int32(table[0][0])
-    for m in range(2):
-        for place in range(4):
-            value = jnp.where((mirror == m) & (q == place), table[m][place], value)
-    return value
-
-
-def gather_kernel(white, cross, rowb, colb, passb, local_sem, row_sem, row2_sem, pass_sem, col_sem, sib_sem,
-                  srow_sem, sy_sem, sr_sem, scol_sem):
+def gather_kernel(white, cross, rowb, colb, steps, local_sem, row_sem, col_sem, sib_sem, srow_sem, sr_sem, scol_sem):
     row, col = lax.axis_index("row"), lax.axis_index("col")
     core, x, y_lo = row % 2, (row // 2) % 4, row // 8
     z, y_hi = col // 2, col % 2
@@ -68,16 +113,18 @@
         return {"row": (yy % 2) * 8 + xx * 2 + cc, "col": zz * 2 + yy // 2}
 
     x_up, x_dn = at((x + 1) % 4, y, z, core), at((x + 3) % 4, y, z, core)
-    y_up, y_dn = at(x, (y + 1) % 4, z, core), at(x, (y + 3) % 4, z, core)
     z_up, z_dn = at(x, y, (z + 1) % 4, core), at(x, y, (z + 3) % 4, core)
     sibling = at(x, y, z, 1 - core)
+    partner = at(x, (y + 2) % 4, z, core)
     pair = at(x, y_hi * 2 + 1 - y_lo, z, core)
     other = at(x, (y + 3 + 2 * y_lo) % 4, z, core)
 
     q = (x + 4 - col % 4) % 4
     mirror = (y_lo + 2 - col // 4) % 2
+    place = mirror * 4 + q
     k = y_lo * 4 + x
     is_root = k == col
+    not_root = jnp.logical_not(is_root)
     feeds = (z == k // 2) & (y_hi != k % 2)
 
     def ident(piece):
@@ -111,9 +158,9 @@
     own = pltpu.make_async_copy(white, rowb.at[ids['E0']], local_sem)
     own.start()
     barrier = pltpu.get_barrier_semaphore()
-    for peer in (x_up, x_dn, y_up, y_dn, z_up, z_dn, sibling):
+    for peer in (x_up, x_dn, pair, other, z_up, z_dn, sibling, partner):
         pl.semaphore_signal(barrier, inc=1, device_id=peer, device_id_type=MESH)
-    pl.semaphore_wait(barrier, 7)
+    pl.semaphore_wait(barrier, 8)
     own.wait()
 
     def root_step(piece, g):
@@ -138,29 +185,13 @@
 
     lax.fori_loop(0, NC, first, 0)
 
-    hf = NF // 2
-
     def y_own(g):
-        src = rowb.at[ids['E0'], pl.ds(g * NF, hf)]
-        remote(src, passb.at[0, g], sy_sem.at[0], pass_sem.at[0, g], y_up)
-        src = rowb.at[ids['E0'], pl.ds(g * NF + hf, hf)]
-        remote(src, passb.at[1, g], sy_sem.at[1], pass_sem.at[1, g], y_dn)
-
-    low_id = z * 2 + (y + 3) % 4 // 2
-    high_id = z * 2 + (y + 1) % 4 // 2
-
-    def y_pass(g):
-        done(passb.at[0, g], pass_sem.at[0, g])
-        remote(passb.at[0, g], rowb.at[low_id, pl.ds(g * NF, hf)], sy_sem.at[2], row_sem.at[low_id, g], y_up)
-        done(passb.at[1, g], pass_sem.at[1, g])
-        remote(passb.at[1, g], rowb.at[high_id, pl.ds(g * NF + hf, hf)], sy_sem.at[3], row2_sem.at[g], y_dn)
+        row_send(6, 'E0', g, partner)
+
+    feed_slot = {'E' + PIECE[n][1]: i for i, n in enumerate(('y0', 'y1'))}
 
     def row_step(piece, g):
-        if piece == 'P0':
-            done(rowb.at[ids[piece], pl.ds(g * NF, hf)], row_sem.at[ids[piece], g])
-            done(rowb.at[ids[piece], pl.ds(g * NF + hf, hf)], row2_sem.at[g])
-        else:
-            done(rowb.at[ids[piece], chunk(g)], row_sem.at[ids[piece], g])
+        done(rowb.at[ids[piece], chunk(g)], row_sem.at[ids[piece], g])
         if piece == 'E3':
             row_send(2, piece, g, z_up)
         if piece == 'P0':
@@ -173,12 +204,11 @@
         def _():
             root_step(piece, g)
 
-        if piece in ('E3', 'E2'):
+        if piece in feed_slot:
             @pl.when(feeds)
             def _():
                 dst = colb.at[core * 8 + ids[piece], chunk(g)]
-                remote(rowb.at[ids[piece], chunk(g)], dst, sr_sem.at[0 if piece == 'E3' else 1],
-                       col_sem.at[ids[piece], g], other)
+                remote(rowb.at[ids[piece], chunk(g)], dst, sr_sem.at[feed_slot[piece]], col_sem.at[ids[piece], g], other)
 
     on_root_row = mirror == 0
     ways = {}
@@ -240,36 +270,57 @@
 
         lax.fori_loop(0, NF // 2, two_bins, 0)
 
-    not_root = jnp.logical_not(is_root)
-    always = row >= 0
-    jobs = [(y_own, 0, 8, always), (y_pass, 2, 8, always)]
-    for piece in ('E3', 'E1', 'P0', 'P1', 'E2', 'P3', 'P2'):
-        jobs.append((functools.partial(row_step, piece), *ROW[piece], always))
-    for name in ('a0', 'b0', 'y0', 'b1', 'a1', 'y1', 'a2', 'b2'):
-        rate, table = COL[name]
-        jobs.append((functools.partial(col_step, name), pick(mirror, q, table), rate, not_root))
-    jobs.append((multiply, *MUL, always))
-
-    def tick(t, state):
-        after = []
-        for (act, start, rate, on), g in zip(jobs, state):
-            due = on & (g < NC) & (t >= start + (rate * g) // 4)
-
-            @pl.when(due)
-            def _(act=act, g=g):
-                act(g)
-
-            after.append(g + due.astype(jnp.int32))
-        return tuple(after)
-
-    lax.fori_loop(0, TICKS, tick, tuple(jnp.int32(0) for _ in jobs))
+    acts = [functools.partial(row_step, n) if n in ROWS else functools.partial(col_step, n) if n in PIECE
+            else y_own for n in ITEMS]
+    for i in range(len(ORDER[0])):
+        word = jnp.int32(ORDER[0][i])
+        for p in range(1, 8):
+            word = jnp.where(place == p, ORDER[p][i], word)
+        steps[i] = word
+
+    def choose(item, g, low, high):
+        if high - low == 1:
+            acts[low](g)
+            return
+        middle = (low + high) // 2
+
+        @pl.when(item < middle)
+        def _():
+            choose(item, g, low, middle)
+
+        @pl.when(item >= middle)
+        def _():
+            choose(item, g, middle, high)
+
+    def three(i, carry):
+        def one(_, word):
+            step = lax.rem(word, 512)
+            item, g = lax.div(step, 16), lax.rem(step, 16)
+
+            @pl.when(item < len(ITEMS))
+            def _():
+                choose(item, g, 0, len(ITEMS))
+
+            return lax.div(word, 512)
+
+        lax.fori_loop(0, 3, one, steps[i])
+        return carry
+
+    lax.fori_loop(0, BEFORE, three, 0)
+
+    def with_multiply(g, carry):
+        multiply(g)
+        start = BEFORE + g * BETWEEN
+        lax.fori_loop(start, start + BETWEEN, three, 0)
+        return carry
+
+    lax.fori_loop(0, NC - 1, with_multiply, 0)
+    multiply(NC - 1)
 
     whole = rowb.at[0]
     half_piece = rowb.at[0, pl.ds(0, F // 2)]
-    for i in range(6):
+    for i in range(7):
         done(whole, srow_sem.at[i])
-    for i in range(4):
-        done(half_piece, sy_sem.at[i])
 
     @pl.when(feeds)
     def _():
@@ -305,15 +356,12 @@
         scratch_shapes=[
             pltpu.VMEM((8, *piece), jnp.bfloat16),
             pltpu.VMEM((16, *piece), jnp.bfloat16),
-            pltpu.VMEM((2, NC, NF // 2, CH, 2 * W), jnp.bfloat16),
+            pltpu.SMEM((len(ORDER[0]),), jnp.int32),
             pltpu.SemaphoreType.DMA,
             pltpu.SemaphoreType.DMA((8, NC)),
-            pltpu.SemaphoreType.DMA((NC,)),
-            pltpu.SemaphoreType.DMA((2, NC)),
             pltpu.SemaphoreType.DMA((8, NC)),
             pltpu.SemaphoreType.DMA((8, NC)),
-            pltpu.SemaphoreType.DMA((6,)),
-            pltpu.SemaphoreType.DMA((4,)),
+            pltpu.SemaphoreType.DMA((7,)),
             pltpu.SemaphoreType.DMA((2,)),
             pltpu.SemaphoreType.DMA((8, 4)),
         ],
@@ -330,42 +378,62 @@
     return [np.kron(m, eye).astype(jnp.bfloat16) for m in (np.cos(angles), -np.sin(angles))]
 
 
-def lag_kernel(mask, cross, even_mat, odd_mat, out):
-    cols = out.shape[2]
-    step = pl.program_id(0)
-    tile_row = lax.axis_index("row") * 2 + step // 8
+def lag_kernel(mask, cross, even_mat, odd_mat, out, buf, sem):
+    rows, cols = out.shape[1], out.shape[2]
+    wide = 256
+    tile_row = lax.axis_index("row") * (rows // BLK)
     tile_col = lax.axis_index("col") * (cols // BLK)
-    scale = jnp.concatenate(
-        [jnp.full((1, BLK), mask[tile_row, tile_col + t].astype(jnp.float32) * (1.0 / math.sqrt(W * F)), jnp.float32)
-         for t in range(cols // BLK)], axis=1)
-    even, odd = [], []
-    for h in range(2):
-        at = step * 2 + h
-        even.append(jnp.dot(even_mat[...], cross[0, at].reshape(F * 8, cols), preferred_element_type=jnp.float32))
-        odd.append(jnp.dot(odd_mat[...], cross[1, at].reshape(F * 8, cols), preferred_element_type=jnp.float32))
-    for m in range(HALF + 1):
-        e = [v[m * 8:m * 8 + 8] for v in even]
-        o = [v[m * 8:m * 8 + 8] for v in odd]
-        if m < HALF:
-            out[HALF + m] = (jnp.concatenate([a + b for a, b in zip(e, o)], 0) * scale).astype(out.dtype)
-        if m > 0:
-            out[HALF - m] = (jnp.concatenate([a - b for a, b in zip(e, o)], 0) * scale).astype(out.dtype)
+
+    def copy(step):
+        here = pl.ds(pl.multiple_of(step * 16, 16), 16)
+        return pltpu.make_async_copy(buf.at[:, here], out.at[:, here], sem.at[step])
+
+    def one(step, carry):
+        here = pl.ds(pl.multiple_of(step * 16, 16), 16)
+        for j in range(cols // wide):
+            span = slice(j * wide, (j + 1) * wide)
+            scale = jnp.concatenate(
+                [jnp.full((1, BLK), mask[tile_row + step // 8, tile_col + t].astype(jnp.float32)
+                          * (1.0 / math.sqrt(W * F)), jnp.float32)
+                 for t in range(j * wide // BLK, (j + 1) * wide // BLK)], axis=1)
+            even, odd = [], []
+            for h in range(2):
+                at = step * 2 + h
+                even.append(jnp.dot(even_mat[...], cross[0, at, :, :, span].reshape(F * 8, wide),
+                                    preferred_element_type=jnp.float32))
+                odd.append(jnp.dot(odd_mat[...], cross[1, at, :, :, span].reshape(F * 8, wide),
+                                   preferred_element_type=jnp.float32))
+            for m in range(HALF + 1):
+                e = [v[m * 8:m * 8 + 8] for v in even]
+                o = [v[m * 8:m * 8 + 8] for v in odd]
+                if m < HALF:
+                    buf[HALF + m, here, span] = (
+                        jnp.concatenate([a + b for a, b in zip(e, o)], 0) * scale).astype(out.dtype)
+                if m > 0:
+                    buf[HALF - m, here, span] = (
+                        jnp.concatenate([a - b for a, b in zip(e, o)], 0) * scale).astype(out.dtype)
+        copy(step).start()
+        return carry
+
+    lax.fori_loop(0, rows // 16, one, 0)
+
+    def finish(step, carry):
+        copy(step).wait()
+        return carry
+
+    lax.fori_loop(0, rows // 16, finish, 0)
 
 
 def lag_transform(cross, tile_mask):
     rows, cols = 256, 512
     even_mat, odd_mat = lag_matrices()
+    vmem = pl.BlockSpec(memory_space=pltpu.VMEM)
     return pl.pallas_call(
         lag_kernel,
-        grid=(rows // 16,),
-        in_specs=[
-            pl.BlockSpec(memory_space=pltpu.SMEM),
-            pl.BlockSpec(memory_space=pltpu.VMEM),
-            pl.BlockSpec(even_mat.shape, lambda i: (0, 0)),
-            pl.BlockSpec(odd_mat.shape, lambda i: (0, 0)),
-        ],
-        out_specs=pl.BlockSpec((LAGS, 16, cols), lambda i: (0, i, 0)),
+        in_specs=[pl.BlockSpec(memory_space=pltpu.SMEM), vmem, vmem, vmem],
+        out_specs=pl.BlockSpec(memory_space=pl.ANY),
         out_shape=jax.ShapeDtypeStruct((LAGS, rows, cols), jnp.bfloat16),
+        scratch_shapes=[pltpu.VMEM((LAGS, rows, cols), jnp.bfloat16), pltpu.SemaphoreType.DMA((rows // 16,))],
         compiler_params=pltpu.CompilerParams(vmem_limit_bytes=30 << 20),
         name="lag_transform",
     )(tile_mask, cross, even_mat, odd_mat)

time: 159 us -> 134 us (0.84); the launches traced: 156 us -> 134 us
  Pallas kernels: 152 us -> 130 us
    pallas_call x1, Pallas kernels: 139 us -> 121 us  [gather_cross(): pl.pallas_call(gather_kernel, out_shape=pltpu.VMEM((2, 32, F // 2, 16, 51...]
    pallas_call x1, Pallas kernels: 13 us -> 9.31 us  [lag_transform(): pl.pallas_call(lag_kernel, in_specs=[pl.BlockSpec(memory_space=pltpu.SMEM...]
where the time goes in v2:
time: 134 us
  Pallas kernels  130 us (97%)
  other arithmetic  3.89 us (3%)
    pallas_call x1, Pallas kernels, gather_cross(): pl.pallas_call(gather_kernel, out_shape=pltpu.VMEM((2, 32, F // 2, 16, 51...  121 us
    pallas_call x1, Pallas kernels, lag_transform(): pl.pallas_call(lag_kernel, in_specs=[pl.BlockSpec(memory_space=pltpu.SMEM...  9.31 us

profile of v2, /device:TPU:27, one launch (start us, length us, event | category | flops | bytes accessed | tf_op | source)
XLA Modules:
  0.0 134.0 jit_solution(8180935899680883127)
XLA Ops:
  0.0 0.7 convert_element_type.8
  0.7 1.5 %convert_element_type.7 = f32[32,32,512]{2,1,0:T(8,128)S(1)} convert(bf16[32,32,512]{2,1,0:T(8,128)(2,1)} %param.5) | non-fusion elementwise | flops 524288 | bytes 3145728 | tf_op jit(solution)/shard_map/convert_element_type | solution.py:89
  2.2 0.2 fusion
  2.3 0.5 multiply_convert_fusion.1
  2.9 1.1 pad_maximum_fusion.white
  3.9 0.0 copy-start
  3.9 0.0 copy-start.1
  3.9 0.0 copy-start.2
  3.9 120.7 %gather_cross.1.cross = bf16[2,32,16,16,512]{4,3,2,1,0:T(8,128)(2,1)S(1)} custom-call(bf16[32,32,512]{2,1,0:T(8,128)(2,1)} %pad_maximum_fusion.white), custom_call_target="tpu_custom_call" | custom-call | tf_op jit(solution)/shard_map/gather_cross/pallas_call | solution.py:351
  124.6 0.0 copy-done
  124.7 0.0 copy-done.1
  124.7 0.0 copy-done.2
  124.7 9.3 %lag_transform.1 = bf16[64,256,512]{2,1,0:T(8,128)(2,1)} custom-call(s32[32,32]{1,0:T(8,128)S(1)} %copy-done.2, bf16[2,32,16,16,512]{4,3,2,1,0:T(8,128)(2,1)S(1)} %gather_cross.1.cross, bf16[264,256]{1,0:T(8,128)(2,1)S(1)} %copy-done.1, bf16[264,256]{1,0:T(8,128)(2,1)S(1)} %copy-done), custom_call_target="tpu_custom_call" | custom-call | tf_op jit(solution)/shard_map/lag_transform/pallas_call | solution.py:431
  (1 shorter events, 0.0 us)
Async XLA Ops:
  3.9 120.7 %copy-start = (bf16[264,256]{1,0:T(8,128)(2,1)S(1)}, bf16[264,256]{1,0:T(8,128)(2,1)}, u32[]{:S(2)}) copy-start(bf16[264,256]{1,0:T(8,128)(2,1)} %constant.12.clone.odd_mat) | copy-start | bytes 405508
  3.9 120.7 %copy-start.1 = (bf16[264,256]{1,0:T(8,128)(2,1)S(1)}, bf16[264,256]{1,0:T(8,128)(2,1)}, u32[]{:S(2)}) copy-start(bf16[264,256]{1,0:T(8,128)(2,1)} %constant.11.clone.even_mat) | copy-start | bytes 405508
  3.9 120.8 %copy-start.2 = (s32[32,32]{1,0:T(8,128)S(1)}, s32[32,32]{1,0:T(8,128)}, u32[]{:S(2)}) copy-start(s32[32,32]{1,0:T(8,128)} %mask.1) | copy-start | bytes 12292

commit v3 on v2

--- a/solution.py
+++ b/solution.py
@@ -19,65 +19,153 @@
 
 NAMES = {'E1': 'a0', 'P0': 'a1', 'E2': 'a2', 'E0': 'b0', 'E3': 'b1', 'P3': 'b2', 'P1': 'y0', 'P2': 'y1'}
 ENTRY = {0: ('y0', 'y1'), 1: ('a0', 'a2'), 2: ('b1', 'a1'), 3: ('b0', 'b2')}
-NC = 8
-BEFORE, BETWEEN = 37, 5
+NC = 16
+BEFORE, BETWEEN = 73, 7
 ORDER = (
-    (8389120, 8675344, 12846097, 795682, 9446947, 13109268, 1321509, 10234918, 1598999, 1867856, 13664864, 25461841,
-     21523011, 134217328, 134217727, 134217727, 134217727, 134217727, 134217727, 134217727, 134217727, 134217727,
-     134217727, 134217727, 134217727, 134217727, 134217727, 134217727, 134217727, 134217727, 134217727, 134217727,
-     134217727, 134217727, 134217727, 134217727, 134217727, 29657171, 134217727, 134217727, 134217727, 134217727,
-     22070326, 134014007, 134217727, 134217727, 134217727, 22579797, 26011206, 134217727, 134217727, 134217727,
-     18656868, 134217332, 134217727, 134217727, 134217727, 134015589, 134217727, 134217727, 134217727, 134217727,
-     134016102, 134217727, 134217727, 134217727, 134217727, 134016615, 134217727, 134217727, 134217727, 134217727),
-    (4194816, 4481056, 12846113, 8922240, 812176, 46155283, 9447553, 13371569, 9710225, 58786994, 9972741, 6096563,
-     47212583, 59049990, 47480912, 1862290, 34958401, 21283042, 35221058, 17613366, 14487232, 38634066, 50913507,
-     21874848, 38897220, 22070501, 42305649, 51700966, 22400661, 26035398, 30181974, 42852551, 54585431, 134217727,
-     134217727, 134217727, 134217727, 18401430, 134062833, 134217727, 134217727, 134217727, 18664100, 39691381,
-     134217458, 134217727, 134217727, 43314278, 31248115, 55437478, 134217727, 134217727, 134064295, 134217727,
-     134217727, 134217727, 134217727, 134064885, 134217727, 134217727, 134217727, 134217727, 134065398, 134217727,
-     134217727, 134217727, 134217727, 134065911, 134217727, 134217727, 134217727, 134217727),
-    (4194816, 4481056, 12846113, 8922288, 4982449, 46727203, 37767188, 46949380, 33835541, 5769908, 47522342,
-     13389335, 47713410, 58753104, 1928835, 13699137, 25264353, 38306897, 17613505, 59271813, 29402306, 21857926,
-     59575921, 38578372, 51759158, 29919330, 51932832, 60089941, 22646420, 54608614, 39118917, 26059495, 42503255,
-     134078674, 134217727, 134217727, 134217727, 26560100, 39381575, 55372902, 31248036, 134217457, 55914196,
-     43625637, 134217458, 134217727, 134217727, 63786711, 134217727, 134217727, 134217727, 134217727, 134217460,
-     134217727, 134217727, 134217727, 134217727, 134217461, 134217727, 134217727, 134217727, 134217727, 134081783,
-     134217727, 134217727, 134217727, 134217727, 134217727, 134217727, 134217727, 134217727, 134217727),
-    (46137856, 12591136, 4473521, 46686722, 13116450, 9266691, 9529363, 13371412, 9792128, 1425429, 10054800,
-     48038422, 13643303, 38126086, 16818368, 34082357, 59278017, 21282947, 14189762, 51167876, 21570627, 14452932,
-     51710691, 35244144, 51947106, 35506757, 29724244, 26027750, 60613840, 54831776, 18394260, 63022195, 134217727,
-     134217727, 134217727, 134217727, 134217727, 39095969, 30453348, 134217457, 134217727, 134217727, 26559699,
-     63547509, 134217727, 134217727, 134217727, 42789990, 31248085, 63810710, 134217727, 134217727, 64073380,
-     134217727, 134217727, 134217727, 134217727, 64309911, 134217727, 134217727, 134217727, 134217727, 64573094,
-     134217727, 134217727, 134217727, 134217727, 134217463, 134217727, 134217727, 134217727, 134217727),
-    (4194816, 8659488, 12846128, 58737682, 9184771, 9447649, 13109424, 46418453, 1376482, 13388822, 46681623,
-     33932806, 59801680, 17088519, 60104883, 47219793, 25494580, 60360259, 60648018, 38068356, 29657171, 62941878,
-     48015458, 29912197, 63245504, 14453333, 18394258, 35513459, 63800419, 22857921, 54585415, 134037748, 134217727,
-     134217727, 134217727, 134217727, 134217727, 54848101, 134038261, 134217727, 134217727, 134217727, 51440742,
-     27084022, 134063223, 134217727, 134217727, 38635255, 134063779, 134217727, 134217727, 134217727, 43100357,
-     55921350, 52276390, 56446613, 134217364, 134217727, 134217727, 134217727, 134217727, 134217727, 134217366,
-     134217727, 134217727, 134217727, 134217727, 134217367, 134217727, 134217727, 134217727, 134217727),
-    (8389120, 4473360, 12846128, 795682, 33564195, 5261362, 13371616, 58993189, 9964161, 46489622, 6049332, 37752034,
-     16818306, 1862322, 34457153, 17343072, 25544849, 46991427, 21523685, 29388468, 34983104, 47482963, 25758951,
-     38330964, 29953718, 42066113, 42304597, 18132067, 48095859, 42526807, 18401475, 51463922, 30707301, 26814195,
-     51767414, 31248036, 134062289, 134217727, 134217727, 134217727, 134217727, 134217727, 51989237, 38882550,
-     52252407, 55158421, 134217727, 134217727, 134217727, 134217727, 134217727, 134217727, 39692950, 134217428,
-     134217727, 134217727, 134217727, 134217727, 134217727, 134217727, 134217727, 134217727, 134217430, 134217727,
-     134217727, 134217727, 134217727, 134217431, 134217727, 134217727, 134217727, 134217727),
-    (8389120, 8675344, 12846097, 795682, 4998706, 46147620, 9725444, 33645077, 10035205, 59097110, 6049332, 46727686,
-     59277392, 17113607, 34170421, 17343072, 25455796, 34457155, 21594167, 59861616, 29664914, 50687108, 50973268,
-     29919330, 51212006, 34924117, 22644967, 18163334, 35512436, 22857413, 42049606, 134217727, 134217727, 134217727,
-     134217727, 134217727, 134217727, 54839494, 26552481, 63236679, 134217727, 134217727, 26840786, 63521910,
-     134217727, 134217727, 134217727, 31248021, 55389347, 134217459, 134217727, 134217727, 43069172, 134217428,
-     134217727, 134217727, 134217727, 55921397, 134217727, 134217727, 134217727, 134217727, 64875686, 134217430,
-     134217727, 134217727, 134217727, 134065831, 134217727, 134217727, 134217727, 134217727),
-    (4194816, 8659488, 12846128, 46154770, 9184771, 9447601, 13109472, 59001365, 5769906, 6055462, 33670183,
-     21063174, 47259712, 59539975, 21282868, 47514178, 17613457, 47776996, 60065874, 34398261, 25788599, 60328531,
-     22094902, 14536305, 29935236, 22381296, 54625413, 30182486, 54888177, 55150663, 30453348, 26545394, 38604405,
-     63761510, 27101907, 55699575, 134037702, 134038229, 134217727, 134217727, 134217727, 134217727, 56174837,
-     56463094, 134217378, 134217727, 134217727, 42856085, 134217727, 134217727, 134217727, 134217727, 134217380,
-     134217727, 134217727, 134217727, 134217727, 39668886, 134217381, 134217727, 134217727, 134217727, 134217727,
-     134217727, 134217727, 134217727, 134217727, 134217383, 134217727, 134217727, 134217727, 134217727),
+    (8389120, 8651792, 8937489, 12846610, 1058339, 13117476, 1321509, 1584166, 13381159, 1847336, 13644329, 6837256,
+     2373163, 13908012, 7625226, 2898990, 8150582, 16818188, 3441233, 14451808, 17605646, 17875512, 18130447,
+     25719366, 22312020, 134012999, 134217727, 134217727, 134217727, 134217727, 134217727, 134217727, 134217727,
+     134217727, 134217727, 134217727, 134217727, 134217727, 134217727, 134217727, 134217727, 134217727, 134217727,
+     134217727, 134217727, 134217727, 134217727, 134217727, 134217727, 134217727, 134217727, 134217727, 134217727,
+     134217727, 134217727, 134217727, 134217727, 134217727, 134217727, 134217727, 134217727, 134217727, 134217727,
+     134217727, 134217727, 134217727, 134217727, 134217727, 134217727, 134217727, 134217727, 134217727, 134217727,
+     15510627, 29659223, 134217727, 134217727, 134217727, 134217727, 134217727, 134217330, 134217727, 134217727,
+     134217727, 134217727, 134217727, 134217727, 23119932, 134217331, 134217727, 134217727, 134217727, 134217727,
+     134217727, 30446169, 134217727, 134217727, 134217727, 134217727, 134217727, 134217727, 19444797, 23906878,
+     134217333, 134217727, 134217727, 134217727, 134217727, 24149579, 26799180, 134217309, 134217727, 134217727,
+     134217727, 134217727, 27061837, 133995614, 134217727, 134217727, 134217727, 134217727, 134217727, 20758120,
+     134217336, 134217727, 134217727, 134217727, 134217727, 134217727, 134017641, 134217727, 134217727, 134217727,
+     134217727, 134217727, 134217727, 134018154, 134217727, 134217727, 134217727, 134217727, 134217727, 134217727,
+     134018667, 134217727, 134217727, 134217727, 134217727, 134217727, 134217727, 134019180, 134217727, 134217727,
+     134217727, 134217727, 134217727, 134217727, 134019693, 134217727, 134217727, 134217727, 134217727, 134217727,
+     134217727, 134020206, 134217727, 134217727, 134217727, 134217727, 134217727, 134217727, 134020719, 134217727,
+     134217727, 134217727, 134217727, 134217727, 134217727),
+    (4194816, 4457504, 8922145, 12648451, 12862995, 13109377, 37767188, 9710256, 13435909, 9972913, 1647156,
+     10235570, 6383235, 1949736, 47213188, 38294041, 47452214, 34886682, 11286198, 35132129, 7433783, 59313708,
+     7696394, 14755373, 12074169, 59576331, 12336826, 3175049, 16818363, 21330068, 3524673, 49575050, 36471890,
+     49814757, 36734560, 21855803, 39067204, 18137792, 60323981, 37260481, 60598466, 51149462, 37530210, 41979588,
+     22663230, 51724912, 39641699, 16634566, 52249687, 18919658, 61681778, 42831987, 23382252, 62206665, 53012553,
+     23714980, 26555509, 53337691, 19445925, 53600374, 31233702, 24458957, 19975335, 63282296, 24694428, 44164303,
+     20233832, 134217424, 134217727, 134217727, 134217727, 134217727, 134217727, 27649705, 54850126, 134217727,
+     134217727, 134217727, 134217727, 134217727, 20763818, 134063226, 134217727, 134217727, 134217727, 134217727,
+     134217727, 28130036, 134063739, 134217727, 134217727, 134217727, 134217727, 134217727, 28437163, 134064252,
+     134217727, 134217727, 134217727, 134217727, 134217727, 28699806, 134064765, 134217727, 134217727, 134217727,
+     134217727, 134217727, 28962476, 134065278, 134217727, 134217727, 134217727, 134217727, 134217727, 29225119,
+     134065791, 134217727, 134217727, 134217727, 134217727, 134217727, 65363117, 134066351, 134217727, 134217727,
+     134217727, 134217727, 134217727, 134066938, 134217727, 134217727, 134217727, 134217727, 134217727, 134217727,
+     134217434, 134217727, 134217727, 134217727, 134217727, 134217727, 134217727, 134067963, 134217727, 134217727,
+     134217727, 134217727, 134217727, 134217727, 134068476, 134217727, 134217727, 134217727, 134217727, 134217727,
+     134217727, 134068989, 134217727, 134217727, 134217727, 134217727, 134217727, 134217727, 134085854, 134217727,
+     134217727, 134217727, 134217727, 134217727, 134217727, 134086367, 134217727, 134217727, 134217727, 134217727,
+     134217727, 134217727),
+    (4194816, 4457504, 4743201, 46138914, 9184817, 5245105, 13198372, 9710208, 33908229, 47205398, 6103046, 13462055,
+     10498178, 38104071, 47993369, 34345012, 48256026, 11286148, 48501472, 11548818, 2648762, 11811461, 35223265,
+     2907166, 14225084, 49569311, 38541538, 49840208, 17080968, 14515725, 17371875, 38804672, 17605728, 14796993,
+     3967114, 25499330, 51153491, 22092005, 15042630, 29410453, 29665989, 51976934, 29928506, 60657294, 52465239,
+     30197391, 60847817, 52998294, 23412969, 15832692, 18957034, 16095349, 26291947, 16313434, 42588365, 54039131,
+     24195135, 26560207, 24457847, 54647882, 31505572, 40477421, 43361355, 26787567, 43624057, 134217456, 134217727,
+     134217727, 134217727, 134217727, 134217727, 134217727, 134217727, 55613543, 32034971, 27610837, 41004109,
+     32283754, 44357288, 134217457, 32561367, 28684458, 63502927, 134217727, 134217727, 134217727, 134217727,
+     28947101, 57228414, 44891759, 134080219, 134217727, 134217727, 134217727, 64075935, 134217727, 134217727,
+     134217727, 134217727, 134217727, 134217727, 64338604, 134217727, 134217727, 134217727, 134217727, 134217727,
+     134217727, 45726893, 134217462, 134217727, 134217727, 134217727, 134217727, 134217727, 64839391, 134217727,
+     134217727, 134217727, 134217727, 134217727, 134217727, 134217464, 134217727, 134217727, 134217727, 134217727,
+     134217727, 134217727, 134217465, 134217727, 134217727, 134217727, 134217727, 134217727, 134217727, 134217466,
+     134217727, 134217727, 134217727, 134217727, 134217727, 134217727, 134217467, 134217727, 134217727, 134217727,
+     134217727, 134217727, 134217727, 66191101, 134217727, 134217727, 134217727, 134217727, 134217727, 134217727,
+     134217727, 134217727, 134217727, 134217727, 134217727, 134217727, 134217727, 134217470, 134217727, 134217727,
+     134217727, 134217727, 134217727, 134217727, 134217727, 134217727, 134217727, 134217727, 134217727, 134217727,
+     134217727),
+    (46137856, 532512, 4473521, 4736178, 46948355, 12854819, 47211524, 47458340, 1321509, 10054707, 1599510,
+     10317440, 10579991, 33931288, 48523783, 37761577, 48762934, 34092074, 11368161, 2433563, 7362748, 14485218,
+     11893258, 14747677, 7888062, 59512466, 8150719, 3175045, 16818368, 21332614, 35506241, 50885645, 38569042,
+     51167246, 15536195, 51422949, 4002372, 18188897, 15804646, 36211910, 52209762, 36556359, 52472381, 36731976,
+     39162467, 52997352, 36994672, 29659851, 26287337, 61446231, 29989464, 54078699, 61924938, 23382671, 42064591,
+     62449872, 23645345, 30777931, 23932655, 20006098, 63022710, 134217727, 134217727, 134217727, 134217727,
+     134217727, 134217727, 134217727, 134217727, 134217727, 134217727, 134217727, 134217727, 55621784, 134217457,
+     134217727, 134217727, 134217727, 134217727, 134217727, 24432291, 55897677, 134079652, 134217727, 134217727,
+     134217727, 134217727, 20495464, 24988374, 40169551, 56423017, 134217459, 134217727, 134217727, 32035994,
+     28134616, 134080635, 134217727, 134217727, 134217727, 134217727, 28397273, 40744060, 64289389, 134217727,
+     134217727, 134217727, 134217727, 28922075, 64600190, 134217727, 134217727, 134217727, 134217727, 134217727,
+     33349276, 134082269, 134217727, 134217727, 134217727, 134217727, 134217727, 44678313, 134217464, 134217727,
+     134217727, 134217727, 134217727, 134217727, 44907231, 134217465, 134217727, 134217727, 134217727, 134217727,
+     134217727, 134083742, 134217727, 134217727, 134217727, 134217727, 134217727, 134217727, 65879724, 134217727,
+     134217727, 134217727, 134217727, 134217727, 134217727, 134084781, 134217727, 134217727, 134217727, 134217727,
+     134217727, 134217727, 134085294, 134217727, 134217727, 134217727, 134217727, 134217727, 134217727, 134085807,
+     134217727, 134217727, 134217727, 134217727, 134217727, 134217727, 134217471, 134217727, 134217727, 134217727,
+     134217727, 134217727, 134217727),
+    (4194816, 4457504, 8922145, 58744835, 1066515, 9447473, 9710130, 59072517, 59264022, 10235398, 46465075, 1855512,
+     46727907, 2118169, 59790362, 7169588, 60035627, 11548802, 47191093, 60316189, 7931573, 37754414, 12336871,
+     47716406, 16818308, 17081064, 34871953, 48006240, 14425321, 48268882, 25547910, 48504388, 21832939, 35418181,
+     61961286, 35694690, 38656699, 22311561, 62486599, 25982064, 62723158, 29659223, 29983424, 36561085, 30191716,
+     23454398, 36730559, 63498313, 15766618, 26576020, 63760987, 16029325, 19970190, 51218550, 26863678, 54599261,
+     31234805, 134037567, 134217727, 134217727, 134217727, 134217727, 134217727, 134217727, 134217727, 134217727,
+     134217727, 134217727, 134217727, 134217727, 134217727, 134217727, 134217727, 24694421, 42331214, 134217425,
+     134217727, 134217727, 134217727, 134217727, 20758120, 51768952, 31773382, 55133432, 134217727, 134217727,
+     134217727, 65336426, 134063779, 134217727, 134217727, 134217727, 134217727, 134217727, 65599083, 28414116,
+     43382396, 134217428, 134217727, 134217727, 134217727, 66124397, 134064839, 134217727, 134217727, 134217727,
+     134217727, 134217727, 66387054, 29207718, 53038846, 134032639, 134217727, 134217727, 134217727, 52756183,
+     56709324, 134033065, 134217727, 134217727, 134217727, 134217727, 44675787, 57514714, 45194411, 134033628,
+     134217727, 134217727, 134217727, 58284765, 134034127, 134217727, 134217727, 134217727, 134217727, 134217727,
+     45989550, 134034587, 134217727, 134217727, 134217727, 134217727, 134217727, 134217727, 134217727, 134217727,
+     134217727, 134217727, 134217727, 134217727, 134035613, 134217727, 134217727, 134217727, 134217727, 134217727,
+     134217727, 134217727, 134217727, 134217727, 134217727, 134217727, 134217727, 134217727, 134036639, 134217727,
+     134217727, 134217727, 134217727, 134217727, 134217727, 134217727, 134217727, 134217727, 134217727, 134217727,
+     134217727, 134217727),
+    (8389120, 8651792, 4736017, 9199619, 1073683, 13117476, 33565221, 13484037, 33827878, 6049286, 10575924,
+     58986008, 34091561, 2212917, 46412842, 11388470, 34345499, 11625616, 59773980, 34617901, 60059315, 2898990,
+     12349585, 34957343, 16818188, 17081062, 3500678, 21525223, 35482690, 25173138, 15323203, 3967059, 25547447,
+     15536197, 18444435, 22140041, 25784892, 50452053, 61936711, 29404221, 36533441, 62186083, 50900542, 23140540,
+     49079368, 30179054, 26286787, 62728281, 30446222, 37609661, 51440218, 23906976, 42306289, 30970972, 42543806,
+     63499851, 24463046, 43093747, 31496294, 27085503, 43592798, 24957172, 43880525, 31759465, 44143349, 32022122,
+     28175562, 64853627, 32561321, 44691607, 53541485, 33086673, 134217424, 134217727, 134217727, 134217727,
+     134217727, 134217727, 134217727, 134217727, 33349369, 44954829, 54109848, 54352123, 55139068, 134217727,
+     134217727, 134217727, 134217727, 134217727, 134217727, 134217727, 134217727, 134217727, 40197373, 40459989,
+     134064382, 134217727, 134217727, 134217727, 134217727, 134217727, 134217727, 134217727, 134217727, 134217727,
+     134217727, 134217727, 56440575, 56210076, 134217727, 134217727, 134217727, 134217727, 134217727, 134217727,
+     134217727, 134217727, 134217727, 134217727, 134217727, 134217727, 134066333, 134217727, 134217727, 134217727,
+     134217727, 134217727, 134217727, 134217727, 134217727, 134217727, 134217727, 134217727, 134217727, 134217727,
+     41793182, 134067421, 134217727, 134217727, 134217727, 134217727, 134217727, 134217727, 134217727, 134217727,
+     134217727, 134217727, 134217727, 134217727, 134217436, 134217727, 134217727, 134217727, 134217727, 134217727,
+     134217727, 134217727, 134217727, 134217727, 134217727, 134217727, 134217727, 134217727, 134069471, 134217727,
+     134217727, 134217727, 134217727, 134217727, 134217727, 134217727, 134217727, 134217727, 134217727, 134217727,
+     134217727, 134217727),
+    (8389120, 8651792, 8937489, 12846610, 13116963, 5261316, 5524019, 13721605, 1584166, 33566247, 10576437,
+     58723864, 6574770, 2163344, 6837302, 7100129, 38015667, 11562626, 2737180, 7625396, 34457144, 2898990, 12413586,
+     3262495, 21064761, 15272000, 3441233, 17369829, 3745463, 21545190, 15560771, 3967110, 21807847, 15797829,
+     22118585, 16109638, 25766074, 61149296, 29665985, 22614715, 49314930, 22906090, 25984583, 36275827, 51425515,
+     30454461, 49883884, 36497992, 26335941, 51965018, 23926975, 62492233, 62729308, 31246989, 24452296, 63017546,
+     31505551, 19742922, 134062231, 134217727, 134217727, 134217727, 134217727, 134217727, 134217727, 134217727,
+     134217727, 134217727, 134217727, 134217727, 134217727, 134217727, 134217727, 26787489, 63542905, 19975921,
+     134062744, 134217727, 134217727, 134217727, 32034978, 134063308, 134217727, 134217727, 134217727, 134217727,
+     134217727, 20239011, 43099853, 32283754, 134080206, 134217727, 134217727, 134217727, 54388843, 32561317,
+     134217428, 134217727, 134217727, 134217727, 134217727, 28658841, 55900751, 134081178, 134217727, 134217727,
+     134217727, 134217727, 56163438, 29183643, 134081663, 134217727, 134217727, 134217727, 134217727, 56447132,
+     65092265, 134217463, 134217727, 134217727, 134217727, 134217727, 134066346, 134217727, 134217727, 134217727,
+     134217727, 134217727, 134217727, 57012894, 134217727, 134217727, 134217727, 134217727, 134217727, 134217727,
+     65623711, 134067451, 134217727, 134217727, 134217727, 134217727, 134217727, 134067884, 134217727, 134217727,
+     134217727, 134217727, 134217727, 134217727, 45463805, 134217468, 134217727, 134217727, 134217727, 134217727,
+     134217727, 134068910, 134217727, 134217727, 134217727, 134217727, 134217727, 134217727, 66960559, 134085855,
+     134217727, 134217727, 134217727, 134217727, 134217727, 134217727, 134217727, 134217727, 134217727, 134217727,
+     134217727, 134217727),
+    (4194816, 4457504, 8922145, 46161923, 1066515, 9447473, 1329685, 46425312, 46681110, 10235398, 6406707, 46927400,
+     10760930, 6881288, 13723690, 11286243, 37841417, 11548801, 59774005, 47733277, 7931109, 38016558, 14179871,
+     60299447, 48267344, 17080963, 60583437, 48530514, 60824708, 38307424, 3967059, 14775429, 61114977, 18425531,
+     35156714, 18655330, 18918076, 49614528, 15324771, 50651222, 19234028, 62197873, 22857787, 50139842, 62448728,
+     19498556, 16066675, 62698085, 30479422, 51412619, 19706982, 51765365, 39182939, 54586444, 63486092, 27102417,
+     31234653, 52274317, 39429875, 20495464, 37589204, 31497823, 64036053, 56160873, 134037705, 134217727, 134217727,
+     134217727, 134217727, 134217727, 134217727, 134217727, 134217727, 53015658, 32298741, 56487115, 39647340,
+     28684535, 134038141, 134217727, 134217378, 134217727, 134217727, 134217727, 134217727, 134217727, 134217727,
+     33086681, 57274572, 53804655, 39958265, 42842276, 134217727, 134217727, 134217727, 134217727, 134217727,
+     134217727, 134217727, 134217727, 134217727, 54115066, 54377723, 43368188, 134217727, 134217727, 134217727,
+     134217727, 134217382, 134217727, 134217727, 134217727, 134217727, 134217727, 134217727, 40499865, 66926334,
+     134217383, 134217727, 134217727, 134217727, 134217727, 134217384, 134217727, 134217727, 134217727, 134217727,
+     134217727, 134217727, 41243804, 134217385, 134217727, 134217727, 134217727, 134217727, 134217727, 134217727,
+     134217727, 134217727, 134217727, 134217727, 134217727, 134217727, 44907692, 134217727, 134217727, 134217727,
+     134217727, 134217727, 134217727, 134217727, 134217727, 134217727, 134217727, 134217727, 134217727, 134217727,
+     45440159, 134217727, 134217727, 134217727, 134217727, 134217727, 134217727, 134217727, 134217727, 134217727,
+     134217727, 134217727, 134217727, 134217727, 134217391, 134217727, 134217727, 134217727, 134217727, 134217727,
+     134217727),
 )
 NF = F // NC
 ROWS = ('E3', 'E1', 'P0', 'P1', 'E2', 'P3', 'P2')
@@ -85,15 +173,27 @@
 PIECE = {n: p for p, n in NAMES.items()}
 
 
-def whiten(spectra, quality):
-    values = spectra.astype(jnp.float32)
-    half_width = values.shape[2] // 2
-    real_part = values[:, :, :half_width]
-    imag_part = values[:, :, half_width:]
-    energy = real_part * real_part + imag_part * imag_part
-    mean_energy = jnp.mean(energy, axis=0, keepdims=True)
-    factor = quality.astype(jnp.float32)[None, :, None] / jnp.sqrt(energy + mean_energy + 1e-06)
-    return jnp.concatenate([real_part * factor, imag_part * factor], axis=2).astype(jnp.bfloat16)
+def whiten(spectra, quality, put):
+    here = lax.broadcasted_iota(jnp.int32, (CH, CH), 0) == lax.broadcasted_iota(jnp.int32, (CH, CH), 1)
+    usable = jnp.sum(jnp.where(here, quality[...].astype(jnp.float32), 0.0), axis=1, keepdims=True)
+
+    def parts(f):
+        values = spectra[f].astype(jnp.float32)
+        real_part, imag_part = values[:, :W], values[:, W:]
+        return real_part, imag_part, real_part * real_part + imag_part * imag_part
+
+    def add(f, total):
+        return total + parts(f)[2]
+
+    mean_energy = lax.fori_loop(0, F, add, jnp.zeros((CH, W), jnp.float32)) / F
+
+    def scale(f, carry):
+        real_part, imag_part, energy = parts(f)
+        factor = usable / jnp.sqrt(energy + mean_energy + 1e-06)
+        put(f, jnp.concatenate([real_part * factor, imag_part * factor], axis=1).astype(jnp.bfloat16))
+        return carry
+
+    lax.fori_loop(0, F, scale, 0)
 
 
 def any_of(q, places):
@@ -103,7 +203,8 @@
     return hit
 
 
-def gather_kernel(white, cross, rowb, colb, steps, local_sem, row_sem, col_sem, sib_sem, srow_sem, sr_sem, scol_sem):
+def gather_kernel(spectra, quality, cross, rowb, colb, steps, local_sem, row_sem, col_sem, sib_sem, srow_sem, sr_sem,
+                  scol_sem, ssib_sem):
     row, col = lax.axis_index("row"), lax.axis_index("col")
     core, x, y_lo = row % 2, (row // 2) % 4, row // 8
     z, y_hi = col // 2, col % 2
@@ -147,21 +248,24 @@
         dst = colb.at[core * 8 + ids[piece], chunk(g)]
         remote(dst if src is None else src, dst, scol_sem.at[slot, way], col_sem.at[ids[piece], g], to)
 
-    def sib_send(src, slot, piece, g):
-        dst = colb.at[core * 8 + ids[piece], chunk(g)]
-        remote(dst if src is None else src, dst, scol_sem.at[slot, 3], sib_sem.at[ids[piece], g], sibling)
-
     def done(ref, sem):
         pltpu.make_async_copy(ref, ref, sem).wait()
 
     slots = {n: i for i, n in enumerate(PIECE)}
-    own = pltpu.make_async_copy(white, rowb.at[ids['E0']], local_sem)
-    own.start()
     barrier = pltpu.get_barrier_semaphore()
     for peer in (x_up, x_dn, pair, other, z_up, z_dn, sibling, partner):
         pl.semaphore_signal(barrier, inc=1, device_id=peer, device_id_type=MESH)
+
+    def put(f, values):
+        rowb[ids['E0'], f] = values
+
+    whiten(spectra, quality, put)
+    for i in range(len(ORDER[0])):
+        word = jnp.int32(ORDER[0][i])
+        for p in range(1, 8):
+            word = jnp.where(place == p, ORDER[p][i], word)
+        steps[i] = word
     pl.semaphore_wait(barrier, 8)
-    own.wait()
 
     def root_step(piece, g):
         name = NAMES[piece]
@@ -170,8 +274,6 @@
             col_send(src, slots[name], 0, piece, g, x_up)
         if name[0] == 'b':
             col_send(src, slots[name], 1, piece, g, x_dn)
-        sib_send(src, slots[name], piece, g)
-        pltpu.make_async_copy(src, colb.at[core * 8 + ids[piece], chunk(g)], col_sem.at[ids[piece], g]).start()
 
     def first(g, carry):
         row_send(0, 'E0', g, z_up)
@@ -243,16 +345,26 @@
         def _():
             col_send(None, slot, 2, piece, g, pair)
 
-        sib_send(None, slot, piece, g)
+    my_half = colb.at[pl.ds(core * 8, 8)]
+
+    def swap(g):
+        mine = my_half.at[:, chunk(g)]
+
+        @pl.when(is_root)
+        def _():
+            pltpu.make_async_copy(rowb.at[:, chunk(g)], mine, local_sem.at[g]).start()
+            remote(rowb.at[:, chunk(g)], mine, ssib_sem, sib_sem.at[g], sibling)
+
+        @pl.when(not_root)
+        def _():
+            remote(mine, mine, ssib_sem, sib_sem.at[g], sibling)
 
     def multiply(g):
         @pl.when(is_root)
         def _():
-            for p in NAMES:
-                done(colb.at[core * 8 + ids[p], chunk(g)], col_sem.at[ids[p], g])
-
-        for p in NAMES:
-            done(colb.at[(1 - core) * 8 + ids[p], chunk(g)], sib_sem.at[ids[p], g])
+            done(my_half.at[:, chunk(g)], local_sem.at[g])
+
+        done(my_half.at[:, chunk(g)], sib_sem.at[g])
 
         def two_bins(h, carry):
             parts = []
@@ -272,11 +384,6 @@
 
     acts = [functools.partial(row_step, n) if n in ROWS else functools.partial(col_step, n) if n in PIECE
             else y_own for n in ITEMS]
-    for i in range(len(ORDER[0])):
-        word = jnp.int32(ORDER[0][i])
-        for p in range(1, 8):
-            word = jnp.where(place == p, ORDER[p][i], word)
-        steps[i] = word
 
     def choose(item, g, low, high):
         if high - low == 1:
@@ -308,10 +415,13 @@
 
     lax.fori_loop(0, BEFORE, three, 0)
 
+    swap(0)
+
     def with_multiply(g, carry):
-        multiply(g)
         start = BEFORE + g * BETWEEN
         lax.fori_loop(start, start + BETWEEN, three, 0)
+        swap(g + 1)
+        multiply(g)
         return carry
 
     lax.fori_loop(0, NC - 1, with_multiply, 0)
@@ -343,31 +453,34 @@
         def _(slot=slot):
             done(whole, scol_sem.at[slot, 2])
 
-        done(whole, scol_sem.at[slot, 3])
-
-
-def gather_cross(white):
+
+    done(my_half, ssib_sem)
+
+
+def gather_cross(spectra, quality):
     piece = (F, CH, 2 * W)
+    vmem = pl.BlockSpec(memory_space=pltpu.VMEM)
     return pl.pallas_call(
         gather_kernel,
         out_shape=pltpu.VMEM((2, 32, F // 2, 16, 512), jnp.bfloat16),
-        in_specs=[pl.BlockSpec(memory_space=pltpu.VMEM)],
-        out_specs=pl.BlockSpec(memory_space=pltpu.VMEM),
+        in_specs=[vmem, vmem],
+        out_specs=vmem,
         scratch_shapes=[
             pltpu.VMEM((8, *piece), jnp.bfloat16),
             pltpu.VMEM((16, *piece), jnp.bfloat16),
             pltpu.SMEM((len(ORDER[0]),), jnp.int32),
-            pltpu.SemaphoreType.DMA,
+            pltpu.SemaphoreType.DMA((NC,)),
             pltpu.SemaphoreType.DMA((8, NC)),
             pltpu.SemaphoreType.DMA((8, NC)),
-            pltpu.SemaphoreType.DMA((8, NC)),
+            pltpu.SemaphoreType.DMA((NC,)),
             pltpu.SemaphoreType.DMA((7,)),
             pltpu.SemaphoreType.DMA((2,)),
-            pltpu.SemaphoreType.DMA((8, 4)),
+            pltpu.SemaphoreType.DMA((8, 3)),
+            pltpu.SemaphoreType.DMA,
         ],
         compiler_params=pltpu.CompilerParams(collective_id=0, has_side_effects=True, vmem_limit_bytes=40 << 20),
         name="gather_cross",
-    )(white)
+    )(spectra, quality.reshape(1, CH))
 
 
 def lag_matrices():
@@ -440,7 +553,7 @@
 
 
 def per_device(spectra, quality, tile_mask):
-    cross = gather_cross(whiten(spectra, quality))
+    cross = gather_cross(spectra, quality)
     return lag_transform(cross, tile_mask)
 
 

time: 134 us -> 127 us (0.948); the launches traced: 134 us -> 125 us
  Pallas kernels: 130 us -> 125 us
  other arithmetic: 3.89 us -> 0 us
    pallas_call x1, Pallas kernels: 121 us -> 115 us  [gather_cross(): pl.pallas_call(gather_kernel, out_shape=pltpu.VMEM((2, 32, F // 2, 16, 51...]
    convert_element_type x2 -> x0, other arithmetic: 2.15 us -> none  [the longest x1 1.49 us: whiten(): values = spectra.astype(jnp.float32)]
where the time goes in v3:
time: 127 us; the launch traced here: 125 us
  Pallas kernels  125 us (98%)
    pallas_call x1, Pallas kernels, gather_cross(): pl.pallas_call(gather_kernel, out_shape=pltpu.VMEM((2, 32, F // 2, 16, 51...  115 us
    pallas_call x1, Pallas kernels, lag_transform(): pl.pallas_call(lag_kernel, in_specs=[pl.BlockSpec(memory_space=pltpu.SMEM...  9.31 us

profile of v3, /device:TPU:27, one launch (start us, length us, event | category | flops | bytes accessed | tf_op | source)
XLA Modules:
  0.0 124.6 jit_solution(14682309460291160826)
XLA Ops:
  0.0 0.0 copy-start
  0.0 0.0 copy-start.1
  0.0 0.0 copy-start.2
  0.0 115.3 %gather_cross.1.cross = bf16[2,32,16,16,512]{4,3,2,1,0:T(8,128)(2,1)S(1)} custom-call(bf16[32,32,512]{2,1,0:T(8,128)(2,1)} %spectra.1, s32[1,32]{1,0:T(1,128)} %bitcast.1), custom_call_target="tpu_custom_call" | custom-call | tf_op jit(solution)/shard_map/gather_cross/pallas_call | solution.py:463
  115.3 0.0 copy-done
  115.3 0.0 copy-done.1
  115.3 0.0 copy-done.2
  115.3 9.3 %lag_transform.1 = bf16[64,256,512]{2,1,0:T(8,128)(2,1)} custom-call(s32[32,32]{1,0:T(8,128)S(1)} %copy-done.2, bf16[2,32,16,16,512]{4,3,2,1,0:T(8,128)(2,1)S(1)} %gather_cross.1.cross, bf16[264,256]{1,0:T(8,128)(2,1)S(1)} %copy-done.1, bf16[264,256]{1,0:T(8,128)(2,1)S(1)} %copy-done), custom_call_target="tpu_custom_call" | custom-call | tf_op jit(solution)/shard_map/lag_transform/pallas_call | solution.py:544
Async XLA Ops:
  0.0 115.3 %copy-start = (bf16[264,256]{1,0:T(8,128)(2,1)S(1)}, bf16[264,256]{1,0:T(8,128)(2,1)}, u32[]{:S(2)}) copy-start(bf16[264,256]{1,0:T(8,128)(2,1)} %constant.5.clone.odd_mat) | copy-start | bytes 405508
  0.0 115.3 %copy-start.1 = (bf16[264,256]{1,0:T(8,128)(2,1)S(1)}, bf16[264,256]{1,0:T(8,128)(2,1)}, u32[]{:S(2)}) copy-start(bf16[264,256]{1,0:T(8,128)(2,1)} %constant.4.clone.even_mat) | copy-start | bytes 405508
  0.0 115.3 %copy-start.2 = (s32[32,32]{1,0:T(8,128)S(1)}, s32[32,32]{1,0:T(8,128)}, u32[]{:S(2)}) copy-start(s32[32,32]{1,0:T(8,128)} %mask.1) | copy-start | bytes 12292

commit v4 on v3

v4 whole, which is shorter than its diff:
```python
import functools
import math

import jax
import jax.numpy as jnp
import numpy as np
from jax import lax
from jax.experimental import pallas as pl
from jax.experimental.pallas import tpu as pltpu
from jax.sharding import PartitionSpec as P

F = 32
LAGS = 64
HALF = LAGS // 2
W = 256
BLK = 128
CH = 32
MESH = pl.DeviceIdType.MESH

NAMES = {'E0': 'a0', 'E3': 'a1', 'E2': 'a2', 'E1': 'b0', 'P0': 'b1', 'P1': 'b2', 'P2': 'y0', 'P3': 'y1'}
ENTRY = {0: ('y0', 'y1'), 1: ('a0', 'a2'), 2: ('a1', 'b1'), 3: ('b2', 'b0')}
NC = 16
BEFORE, BETWEEN = 68, 7
ORDER = (
    (8389120, 4473360, 8937474, 811538, 9446947, 9701396, 9987093, 10226198, 10511895, 10751000, 11013657, 11298842,
     11538459, 7625244, 12063285, 8150558, 16818186, 21239350, 17350721, 21502007, 17875523, 18130445, 3705912,
     18655330, 134217328, 134217727, 134217727, 134217727, 134217727, 134217727, 134217727, 134217727, 134217727,
     134217727, 134217727, 134217727, 134217727, 134217727, 134217727, 134217727, 134217727, 134217727, 134217727,
     134217727, 134217727, 134217727, 134217727, 134217727, 134217727, 134217727, 134217727, 134217727, 134217727,
     134217727, 134217727, 134217727, 134217727, 134217727, 134217727, 134217727, 134217727, 134217727, 134217727,
     134217727, 134217727, 134217727, 134217727, 134217727, 22311439, 29666403, 134217727, 134217727, 134217727,
     134217727, 134217727, 134014024, 134217727, 134217727, 134217727, 134217727, 134217727, 134217727, 30191162,
     134217727, 134217727, 134217727, 134217727, 134217727, 134217727, 15511652, 30454345, 134217727, 134217727,
     134217727, 134217727, 134217727, 15774837, 133993573, 134217727, 134217727, 134217727, 134217727, 134217727,
     30964315, 24149067, 19970662, 134217727, 134217727, 134217727, 134217727, 16554615, 20500062, 134217727,
     134217727, 134217727, 134217727, 134217727, 27324511, 134217295, 134217727, 134217727, 134217727, 134217727,
     134217727, 134017641, 134217727, 134217727, 134217727, 134217727, 134217727, 134217727, 134018154, 134217727,
     134217727, 134217727, 134217727, 134217727, 134217727, 134018667, 134217727, 134217727, 134217727, 134217727,
     134217727, 134217727, 134019180, 134217727, 134217727, 134217727, 134217727, 134217727, 134217727, 134019693,
     134217727, 134217727, 134217727, 134217727, 134217727, 134217727, 33087086, 134217727, 134217727, 134217727,
     134217727, 134217727, 134217727, 134217343, 134217727, 134217727, 134217727, 134217727, 134217727, 134217727),
    (33554944, 33832976, 541201, 4785200, 811554, 9184899, 5310514, 34867236, 13388309, 9972870, 6098437, 13721639,
     6361328, 46402600, 10760841, 1958592, 11023498, 36529205, 50615835, 36704498, 14178332, 7674547, 47190573,
     37348919, 37510174, 2645535, 37873845, 50888784, 38016568, 47743569, 17376501, 21545143, 15068172, 51152531,
     17901665, 15298573, 39102199, 25784901, 3706006, 48789240, 18689620, 22382607, 15786136, 65352379, 18918499,
     49362033, 16070394, 22857917, 65856585, 23169692, 49866397, 41464382, 50198644, 16596581, 54585930, 41989373,
     42251974, 30971646, 42514641, 26846463, 134070435, 134217727, 134217727, 134217727, 134217727, 134217727,
     134217727, 134217727, 24440396, 59084452, 134217727, 134217727, 134217727, 134217727, 134217727, 27109029,
     31496798, 134071462, 134217727, 134217727, 134217727, 134217727, 43826900, 134217443, 134217727, 134217727,
     134217727, 134217727, 134217727, 31759573, 52514920, 56185449, 59831375, 134217727, 134217727, 134217727,
     56448106, 32331371, 134073033, 134217727, 134217727, 134217727, 134217727, 32594028, 45406936, 60396669,
     134217727, 134217727, 134217727, 134217727, 33119342, 134074073, 134217727, 134217727, 134217727, 134217727,
     134217727, 33381999, 134074571, 134217727, 134217727, 134217727, 134217727, 134217727, 134075098, 134217727,
     134217727, 134217727, 134217727, 134217727, 134217727, 134075596, 134217727, 134217727, 134217727, 134217727,
     134217727, 134217727, 57530061, 134217727, 134217727, 134217727, 134217727, 134217727, 134217727, 134076636,
     134217727, 134217727, 134217727, 134217727, 134217727, 134217727, 58055374, 134217727, 134217727, 134217727,
     134217727, 134217727, 134217727, 58302190, 134217727, 134217727, 134217727, 134217727, 134217727, 134217727,
     134078175, 134217727, 134217727, 134217727, 134217727, 134217727, 134217727),
    (4194816, 8659488, 4743170, 33579554, 9184771, 9447553, 1074306, 9710256, 5857923, 1378342, 6127667, 46729767,
     1593368, 6652550, 35416105, 6819507, 35774506, 11286196, 2167349, 47470620, 7673073, 2458669, 12074123,
     63466678, 12336780, 36967607, 51150928, 2911987, 37257809, 37520568, 25290937, 17569874, 48832568, 17875701,
     3508369, 38308435, 15068347, 49340500, 22289555, 18446996, 25697905, 39089399, 29928645, 65109142, 39614039,
     18710131, 23119512, 54556788, 23409401, 40471669, 23721021, 31012561, 18925630, 31323858, 16561820, 52247292,
     66359900, 24487582, 55656056, 19446885, 55967392, 66667129, 19709640, 134070434, 134217727, 134217727,
     134217727, 134217727, 32034006, 27111075, 52774988, 43316840, 59298520, 53038157, 59045994, 134217727,
     134217727, 134217727, 134217727, 134217727, 134217727, 134217727, 28153511, 44080253, 44357849, 28638412,
     59618474, 134217727, 134217727, 33332846, 59873963, 134217727, 134217727, 134217727, 134217727, 134217727,
     57497711, 134217445, 134217727, 134217727, 134217727, 134217727, 134217727, 45718701, 134073564, 134217727,
     134217727, 134217727, 134217727, 134217727, 54353629, 134217447, 134217727, 134217727, 134217727, 134217727,
     134217727, 60931806, 134217727, 134217727, 134217727, 134217727, 134217727, 134217727, 134217449, 134217727,
     134217727, 134217727, 134217727, 134217727, 134217727, 134075627, 134217727, 134217727, 134217727, 134217727,
     134217727, 134217727, 134217727, 134217727, 134217727, 134217727, 134217727, 134217727, 134217727, 134217452,
     134217727, 134217727, 134217727, 134217727, 134217727, 134217727, 134217453, 134217727, 134217727, 134217727,
     134217727, 134217727, 134217727, 134217454, 134217727, 134217727, 134217727, 134217727, 134217727, 134217727,
     134217455, 134217727, 134217727, 134217727, 134217727, 134217727, 134217727),
    (8389120, 4473360, 8937474, 46162450, 4998659, 9462961, 33652756, 5523972, 33907763, 50605094, 13698053,
     46935591, 10608771, 47189016, 6574724, 63269429, 11013765, 35226650, 47724075, 11538674, 48000028, 7625351,
     2459191, 12183176, 36007966, 63979055, 36270602, 14712912, 36443834, 51413585, 36825657, 25261634, 36968530,
     49409091, 15239265, 3504782, 64784979, 3771023, 18393278, 37875771, 50126946, 4006485, 38400720, 15786567,
     25996486, 38566514, 65580753, 30254228, 39091272, 30453959, 55389435, 39629412, 23625428, 66120265, 31011029,
     40210685, 66622555, 26555606, 66907740, 24458967, 19775689, 56703096, 41209057, 52992094, 27081849, 53331039,
     56966733, 134037731, 53517416, 134217377, 134217727, 134217727, 134217727, 134217727, 134217727, 32093289,
     42584143, 134217727, 134217727, 134217727, 134217727, 134217727, 60136042, 134217379, 134217727, 134217727,
     134217727, 134217727, 134217727, 57472619, 134217380, 134217727, 134217727, 134217727, 134217727, 134217727,
     54065260, 134217381, 134217727, 134217727, 134217727, 134217727, 134217727, 57735789, 33086694, 134217382,
     134217727, 134217727, 134217727, 134217727, 33349341, 134041319, 134217727, 134217727, 134217727, 134217727,
     134217727, 44159183, 134217727, 134217727, 134217727, 134217727, 134217727, 134217727, 58544862, 134217449,
     134217727, 134217727, 134217727, 134217727, 134217727, 134075562, 134217727, 134217727, 134217727, 134217727,
     134217727, 134217727, 134076075, 134217727, 134217727, 134217727, 134217727, 134217727, 134217727, 134076588,
     134217727, 134217727, 134217727, 134217727, 134217727, 134217727, 62217389, 134217727, 134217727, 134217727,
     134217727, 134217727, 134217727, 134077615, 134217727, 134217727, 134217727, 134217727, 134217727, 134217727,
     134217455, 134217727, 134217727, 134217727, 134217727, 134217727, 134217727),
    (4194816, 8659488, 8922114, 811568, 62932499, 63195156, 9710084, 5832754, 1434662, 10235521, 6416048, 13372456,
     10760834, 1960113, 13653018, 11286147, 34728626, 11548680, 11811574, 34869939, 12074231, 47284277, 2645535,
     50662648, 35422288, 2976505, 14189137, 17350792, 65542326, 35948114, 17875707, 14424759, 36211283, 48270588,
     22070286, 14809794, 36495431, 66592441, 26024021, 29666490, 51248781, 29913672, 58793047, 26310259, 59019864,
     30454415, 38084666, 30767330, 15563354, 23893093, 38389366, 15825995, 59844188, 19970662, 31293124, 60062285,
     41991376, 134217727, 134217727, 134217727, 134217727, 134217727, 134217727, 134217727, 134217727, 134217727,
     134217727, 134217727, 38837351, 24935654, 54849685, 134038079, 134217727, 134217727, 134217727, 20762855,
     134038738, 134217727, 134217727, 134217727, 134217727, 134217727, 51704425, 27870952, 134063738, 134217727,
     134217727, 134217727, 134217727, 28126953, 61418619, 32561316, 134217428, 134217727, 134217727, 134217727,
     28658411, 134064765, 134217727, 134217727, 134217727, 134217727, 134217727, 28914412, 33151640, 56155814,
     134057198, 134217727, 134217727, 134217727, 43900631, 44105432, 56971930, 44676251, 57497244, 134057644,
     134217727, 41269421, 41508061, 41794735, 134058207, 134217727, 134217727, 134217727, 134217417, 134217727,
     134217727, 134217727, 134217727, 134217727, 134217727, 134217418, 134217727, 134217727, 134217727, 134217727,
     134217727, 134217727, 134217419, 134217727, 134217727, 134217727, 134217727, 134217727, 134217727, 134217420,
     134217727, 134217727, 134217727, 134217727, 134217727, 134217727, 134217421, 134217727, 134217727, 134217727,
     134217727, 134217727, 134217727, 134217422, 134217727, 134217727, 134217727, 134217727, 134217727, 134217727,
     134217423, 134217727, 134217727, 134217727, 134217727, 134217727, 134217727),
    (8389120, 4473360, 4736002, 811568, 33564195, 33826852, 5523972, 10084402, 1377302, 6049521, 10552883, 63441944,
     34615849, 11013808, 13755930, 34879019, 50335921, 35141676, 7625460, 64324105, 12127797, 64578590, 2637359,
     21063304, 64777280, 17080843, 65104009, 21545026, 50926604, 14545475, 47482977, 47717003, 65571411, 25790092,
     3798598, 18655288, 4004535, 66117717, 37821497, 18918499, 37616241, 15299256, 19181156, 38141042, 15829051,
     66905688, 23362234, 38387828, 19430501, 38631029, 49315418, 31048283, 24193099, 49597666, 31277205, 51690060,
     39437985, 24694434, 59830349, 24987326, 43069119, 27325006, 43331813, 134062185, 134217727, 134217727,
     134217727, 134217727, 20794566, 60347514, 28135065, 60634235, 32561320, 134217425, 134217727, 134217426,
     134217727, 134217727, 134217727, 134217727, 134217727, 134217727, 32823977, 44683419, 40959086, 29185769,
     134063743, 134217727, 134217727, 52254954, 134217428, 134217727, 134217727, 134217727, 134217727, 134217727,
     61684397, 61947054, 134064815, 134217727, 134217727, 134217727, 134217727, 56180461, 134217727, 134217727,
     134217727, 134217727, 134217727, 134217727, 52813000, 134065903, 134217727, 134217727, 134217727, 134217727,
     134217727, 134217432, 134217727, 134217727, 134217727, 134217727, 134217727, 134217727, 53327050, 134217433,
     134217727, 134217727, 134217727, 134217727, 134217727, 134217727, 134217727, 134217727, 134217727, 134217727,
     134217727, 134217727, 53844188, 134217435, 134217727, 134217727, 134217727, 134217727, 134217727, 134217727,
     134217727, 134217727, 134217727, 134217727, 134217727, 134217727, 54369502, 134217437, 134217727, 134217727,
     134217727, 134217727, 134217727, 134217727, 134217727, 134217727, 134217727, 134217727, 134217727, 134217727,
     134217439, 134217727, 134217727, 134217727, 134217727, 134217727, 134217727),
    (8389120, 4473360, 8937474, 811538, 13116963, 1058852, 5524019, 5786752, 13697541, 46149159, 62926888, 10814470,
     50422297, 1862385, 34354218, 7100146, 2164929, 11625526, 11920924, 14509597, 12126729, 35252254, 47201839,
     21096970, 47476800, 35395266, 17080889, 17371382, 21545142, 17690124, 25498307, 15298116, 18130445, 22091000,
     3764336, 22409787, 29658256, 4003513, 65566818, 22616209, 51475570, 16035579, 66132595, 26027079, 37283928,
     66418238, 38595161, 49329295, 26274964, 66616904, 39190135, 51739227, 49844828, 39383133, 26554080, 50107486,
     59060345, 40146527, 134037712, 134217727, 134217727, 134217727, 134217727, 134217727, 134217727, 134217727,
     134217727, 134217727, 51967078, 27116753, 55129164, 134217377, 134217727, 134217727, 134217727, 40695400,
     134038755, 134217727, 134217727, 134217727, 134217727, 134217727, 20265065, 134039251, 134217727, 134217727,
     134217727, 134217727, 134217727, 52230250, 28166356, 20527741, 134039765, 134217727, 134217727, 134217727,
     56179820, 28638373, 134072991, 134217727, 134217727, 134217727, 134217727, 20765862, 56426184, 52747943,
     134073560, 134217727, 134217727, 134217727, 44151498, 134074059, 134217727, 134217727, 134217727, 134217727,
     134217727, 57252009, 57514666, 134217448, 134217727, 134217727, 134217727, 134217727, 134075086, 134217727,
     134217727, 134217727, 134217727, 134217727, 134217727, 45201579, 61462223, 134217727, 134217727, 134217727,
     134217727, 134217727, 134217727, 134217727, 134217727, 134217727, 134217727, 134217727, 134217727, 58284765,
     45996718, 134076639, 134217727, 134217727, 134217727, 134217727, 134217727, 134217727, 134217727, 134217727,
     134217727, 134217727, 134217727, 134077679, 134217727, 134217727, 134217727, 134217727, 134217727, 134217727,
     134217727, 134217727, 134217727, 134217727, 134217727, 134217727, 134217727),
    (4194816, 8659488, 8922114, 811568, 13125139, 1067028, 9710256, 9972976, 46402099, 10235633, 6357044, 63441960,
     10760882, 1862273, 63722522, 7144627, 2222123, 11548864, 34368692, 2382365, 64318145, 14441502, 8252548,
     47715375, 16818309, 21239543, 48001089, 17428614, 21545017, 17662988, 25522425, 3477060, 18130568, 15299322,
     3740355, 48794708, 65855586, 36206165, 49149967, 15786567, 37878358, 22864995, 30242955, 49675409, 36745288,
     30440077, 51425892, 49839359, 30708314, 31047826, 37584526, 19474011, 54641215, 31242341, 54903956, 19737181,
     59614328, 55364805, 39360606, 59877497, 39632487, 39955021, 27372773, 56462414, 32099433, 56701519, 134037610,
     134217727, 28160666, 42323579, 134217727, 134217727, 134217727, 134217727, 134217727, 60881004, 28685467,
     134038653, 134217727, 134217727, 134217727, 134217727, 33086620, 57511657, 61406831, 134217379, 134217727,
     134217727, 134217727, 134217380, 134217727, 134217727, 134217727, 134217727, 134217727, 134217727, 61684444,
     61979294, 62241951, 134217381, 134217727, 134217727, 134217727, 134040799, 134217727, 134217727, 134217727,
     134217727, 134217727, 134217727, 52813000, 44143855, 134217383, 134217727, 134217727, 134217727, 134217727,
     134217727, 134217727, 134217727, 134217727, 134217727, 134217727, 134217727, 53581482, 134042284, 134217727,
     134217727, 134217727, 134217727, 134217727, 134217727, 134217727, 134217727, 134217727, 134217727, 134217727,
     134217727, 54090957, 134217387, 134217727, 134217727, 134217727, 134217727, 134217727, 134217727, 134217727,
     134217727, 134217727, 134217727, 134217727, 134217727, 134044367, 134217727, 134217727, 134217727, 134217727,
     134217727, 134217727, 134217727, 134217727, 134217727, 134217727, 134217727, 134217727, 134217727, 134217391,
     134217727, 134217727, 134217727, 134217727, 134217727, 134217727),
)
NF = F // NC
ROWS = ('E3', 'E1', 'P0', 'P1', 'E2', 'P3', 'P2')
ITEMS = ('own', *ROWS, *sorted(NAMES.values()))
PIECE = {n: p for p, n in NAMES.items()}


def whiten(spectra, quality, put):
    here = lax.broadcasted_iota(jnp.int32, (CH, CH), 0) == lax.broadcasted_iota(jnp.int32, (CH, CH), 1)
    usable = jnp.sum(jnp.where(here, quality[...].astype(jnp.float32), 0.0), axis=1, keepdims=True)

    def parts(f):
        values = spectra[f].astype(jnp.float32)
        real_part, imag_part = values[:, :W], values[:, W:]
        return real_part, imag_part, real_part * real_part + imag_part * imag_part

    def add(f, total):
        return total + parts(f)[2]

    mean_energy = lax.fori_loop(0, F, add, jnp.zeros((CH, W), jnp.float32), unroll=4) / F

    def scale(f, carry):
        real_part, imag_part, energy = parts(f)
        factor = usable / jnp.sqrt(energy + mean_energy + 1e-06)
        put(f, jnp.concatenate([real_part * factor, imag_part * factor], axis=1).astype(jnp.bfloat16))
        return carry

    lax.fori_loop(0, F, scale, 0, unroll=4)


def any_of(q, places):
    hit = q < 0
    for place in places:
        hit = hit | (q == place)
    return hit


def gather_kernel(spectra, quality, cross, rowb, colb, steps, local_sem, row_sem, col_sem, sib_sem, srow_sem, sr_sem,
                  scol_sem, ssib_sem):
    row, col = lax.axis_index("row"), lax.axis_index("col")
    core, x, y_lo = row % 2, (row // 2) % 4, row // 8
    z, y_hi = col // 2, col % 2
    y = y_hi * 2 + y_lo

    def at(xx, yy, zz, cc):
        return {"row": (yy % 2) * 8 + xx * 2 + cc, "col": zz * 2 + yy // 2}

    x_up, x_dn = at((x + 1) % 4, y, z, core), at((x + 3) % 4, y, z, core)
    z_up, z_dn = at(x, y, (z + 1) % 4, core), at(x, y, (z + 3) % 4, core)
    sibling = at(x, y, z, 1 - core)
    partner = at(x, (y + 2) % 4, z, core)
    pair = at(x, y_hi * 2 + 1 - y_lo, z, core)
    other = at(x, (y + 3 + 2 * y_lo) % 4, z, core)

    q = (x + 4 - col % 4) % 4
    mirror = (y_lo + 2 - col // 4) % 2
    place = mirror * 4 + q
    k = y_lo * 4 + x
    is_root = k == col
    not_root = jnp.logical_not(is_root)
    feeds = (z == k // 2) & (y_hi != k % 2)

    def ident(piece):
        half = y_hi if piece[0] == 'E' else 1 - y_hi
        return ((z + int(piece[1])) % 4) * 2 + half

    ids = {p: ident(p) for p in NAMES}

    def chunk(g):
        return pl.ds(g * NF, NF)

    def remote(src, dst, send, recv, to):
        pltpu.make_async_remote_copy(src, dst, send, recv, device_id=to, device_id_type=MESH).start()

    def row_send(slot, piece, g, to):
        part = rowb.at[ids[piece], chunk(g)]
        remote(part, part, srow_sem.at[slot], row_sem.at[ids[piece], g], to)

    def col_send(src, slot, way, piece, g, to):
        dst = colb.at[core * 8 + ids[piece], chunk(g)]
        remote(dst if src is None else src, dst, scol_sem.at[slot, way], col_sem.at[ids[piece], g], to)

    def done(ref, sem):
        pltpu.make_async_copy(ref, ref, sem).wait()

    slots = {n: i for i, n in enumerate(PIECE)}
    barrier = pltpu.get_barrier_semaphore()
    for peer in (x_up, x_dn, pair, other, z_up, z_dn, sibling, partner):
        pl.semaphore_signal(barrier, inc=1, device_id=peer, device_id_type=MESH)

    def put(f, values):
        rowb[ids['E0'], f] = values

    whiten(spectra, quality, put)
    for i in range(len(ORDER[0])):
        word = jnp.int32(ORDER[0][i])
        for p in range(1, 8):
            word = jnp.where(place == p, ORDER[p][i], word)
        steps[i] = word
    pl.semaphore_wait(barrier, 8)

    def root_step(piece, g):
        name = NAMES[piece]
        src = rowb.at[ids[piece], chunk(g)]
        if name[0] == 'a':
            col_send(src, slots[name], 0, piece, g, x_up)
        if name[0] == 'b':
            col_send(src, slots[name], 1, piece, g, x_dn)

    def first(g, carry):
        row_send(0, 'E0', g, z_up)
        row_send(1, 'E0', g, z_dn)

        @pl.when(is_root)
        def _():
            root_step('E0', g)

        return carry

    lax.fori_loop(0, NC, first, 0)

    def y_own(g):
        row_send(6, 'E0', g, partner)

    feed_slot = {'E' + PIECE[n][1]: i for i, n in enumerate(('y0', 'y1'))}

    def row_step(piece, g):
        done(rowb.at[ids[piece], chunk(g)], row_sem.at[ids[piece], g])
        if piece == 'E3':
            row_send(2, piece, g, z_up)
        if piece == 'P0':
            row_send(3, piece, g, z_up)
            row_send(4, piece, g, z_dn)
        if piece == 'P1':
            row_send(5, piece, g, z_dn)

        @pl.when(is_root)
        def _():
            root_step(piece, g)

        if piece in feed_slot:
            @pl.when(feeds)
            def _():
                dst = colb.at[core * 8 + ids[piece], chunk(g)]
                remote(rowb.at[ids[piece], chunk(g)], dst, sr_sem.at[feed_slot[piece]], col_sem.at[ids[piece], g], other)

    on_root_row = mirror == 0
    ways = {}
    for name in slots:
        up = on_root_row & any_of(q, (1, 2)) & (name[0] == 'a')
        down = on_root_row & any_of(q, (3, 2)) & (name[0] == 'b')
        over = jnp.where(on_root_row, any_of(q, [p for p in (1, 2, 3) if name in ENTRY[p]]),
                         any_of(q, (1, 2, 3)) & (name[0] == 'y'))
        enters = [p for p in range(4) if name in ENTRY[p]][0]
        order = ENTRY[enters].index(name)
        mirrored = mirror == 1
        full = mirrored & (q == enters)
        up_half = mirrored & (q == (enters + 1) % 4)
        down_half = mirrored & (q == (enters + 3) % 4)
        ways[name] = (up | full, up_half, down | full, down_half, over, order)

    def col_step(name, g):
        piece = PIECE[name]
        slot = slots[name]
        done(colb.at[core * 8 + ids[piece], chunk(g)], col_sem.at[ids[piece], g])
        up, up_half, down, down_half, over, order = ways[name]

        @pl.when(up | (up_half & (g % 2 == order)))
        def _():
            col_send(None, slot, 0, piece, g, x_up)

        @pl.when(down | (down_half & (g % 2 != order)))
        def _():
            col_send(None, slot, 1, piece, g, x_dn)

        @pl.when(over)
        def _():
            col_send(None, slot, 2, piece, g, pair)

    my_half = colb.at[pl.ds(core * 8, 8)]

    def swap(g):
        mine = my_half.at[:, chunk(g)]

        @pl.when(is_root)
        def _():
            pltpu.make_async_copy(rowb.at[:, chunk(g)], mine, local_sem.at[g]).start()
            remote(rowb.at[:, chunk(g)], mine, ssib_sem, sib_sem.at[g], sibling)

        @pl.when(not_root)
        def _():
            remote(mine, mine, ssib_sem, sib_sem.at[g], sibling)

    def multiply(g):
        @pl.when(is_root)
        def _():
            done(my_half.at[:, chunk(g)], local_sem.at[g])

        done(my_half.at[:, chunk(g)], sib_sem.at[g])

        def two_bins(h, carry):
            parts = []
            for e in range(2):
                f = g * NF + h * 2 + e
                lhs = rowb[:, f].reshape(8 * CH, 2 * W)
                turned = jnp.concatenate([lhs[:, W:], -lhs[:, :W]], axis=1)
                rhs = colb[:, f].reshape(16 * CH, 2 * W)
                parts.append(lax.dot_general(jnp.concatenate([lhs, turned], axis=0), rhs, (((1,), (1,)), ((), ())),
                                             preferred_element_type=jnp.float32))
            for c in range(2):
                both = [p[c * 256:(c + 1) * 256].reshape(32, 8, 512) for p in parts]
                cross[c, :, g * (NF // 2) + h] = jnp.concatenate(both, axis=1).astype(jnp.bfloat16)
            return carry

        lax.fori_loop(0, NF // 2, two_bins, 0)

    acts = [functools.partial(row_step, n) if n in ROWS else functools.partial(col_step, n) if n in PIECE
            else y_own for n in ITEMS]

    def choose(item, g, low, high):
        if high - low == 1:
            acts[low](g)
            return
        middle = (low + high) // 2

        @pl.when(item < middle)
        def _():
            choose(item, g, low, middle)

        @pl.when(item >= middle)
        def _():
            choose(item, g, middle, high)

    def three(i, carry):
        def one(_, word):
            step = lax.rem(word, 512)
            item, g = lax.div(step, 16), lax.rem(step, 16)

            @pl.when(item < len(ITEMS))
            def _():
                choose(item, g, 0, len(ITEMS))

            return lax.div(word, 512)

        lax.fori_loop(0, 3, one, steps[i])
        return carry

    lax.fori_loop(0, BEFORE, three, 0)

    swap(0)

    def with_multiply(g, carry):
        start = BEFORE + g * BETWEEN
        lax.fori_loop(start, start + BETWEEN, three, 0)
        swap(g + 1)
        multiply(g)
        return carry

    lax.fori_loop(0, NC - 1, with_multiply, 0)
    multiply(NC - 1)

    whole = rowb.at[0]
    half_piece = rowb.at[0, pl.ds(0, F // 2)]
    for i in range(7):
        done(whole, srow_sem.at[i])

    @pl.when(feeds)
    def _():
        done(whole, sr_sem.at[0])
        done(whole, sr_sem.at[1])

    for name in slots:
        up, up_half, down, down_half, over, _ = ways[name]
        slot = slots[name]
        for way, full, part, letter in ((0, up, up_half, 'a'), (1, down, down_half, 'b')):
            @pl.when(jnp.where(is_root, name[0] == letter, full))
            def _(slot=slot, way=way):
                done(whole, scol_sem.at[slot, way])

            @pl.when(not_root & part)
            def _(slot=slot, way=way):
                done(half_piece, scol_sem.at[slot, way])

        @pl.when(not_root & over)
        def _(slot=slot):
            done(whole, scol_sem.at[slot, 2])


    done(my_half, ssib_sem)


def gather_cross(spectra, quality):
    piece = (F, CH, 2 * W)
    vmem = pl.BlockSpec(memory_space=pltpu.VMEM)
    return pl.pallas_call(
        gather_kernel,
        out_shape=pltpu.VMEM((2, 32, F // 2, 16, 512), jnp.bfloat16),
        in_specs=[vmem, vmem],
        out_specs=vmem,
        scratch_shapes=[
            pltpu.VMEM((8, *piece), jnp.bfloat16),
            pltpu.VMEM((16, *piece), jnp.bfloat16),
            pltpu.SMEM((len(ORDER[0]),), jnp.int32),
            pltpu.SemaphoreType.DMA((NC,)),
            pltpu.SemaphoreType.DMA((8, NC)),
            pltpu.SemaphoreType.DMA((8, NC)),
            pltpu.SemaphoreType.DMA((NC,)),
            pltpu.SemaphoreType.DMA((7,)),
            pltpu.SemaphoreType.DMA((2,)),
            pltpu.SemaphoreType.DMA((8, 3)),
            pltpu.SemaphoreType.DMA,
        ],
        compiler_params=pltpu.CompilerParams(collective_id=0, has_side_effects=True, vmem_limit_bytes=40 << 20),
        name="gather_cross",
    )(spectra, quality.reshape(1, CH))


def lag_matrices():
    lag = np.arange(HALF + 1, dtype=np.float32)
    frequency = np.arange(F, dtype=np.float32) + np.float32(1.0)
    angles = np.float32(2.0 * math.pi) * frequency[None, :] * lag[:, None] / np.float32(2.0 * LAGS)
    eye = np.eye(8, dtype=np.float32)
    return [np.kron(m, eye).astype(jnp.bfloat16) for m in (np.cos(angles), -np.sin(angles))]


def lag_kernel(mask, cross, even_mat, odd_mat, out, buf, sem):
    rows, cols = out.shape[1], out.shape[2]
    wide = 256
    tile_row = lax.axis_index("row") * (rows // BLK)
    tile_col = lax.axis_index("col") * (cols // BLK)

    def copy(step):
        here = pl.ds(pl.multiple_of(step * 16, 16), 16)
        return pltpu.make_async_copy(buf.at[:, here], out.at[:, here], sem.at[step])

    def one(step, carry):
        here = pl.ds(pl.multiple_of(step * 16, 16), 16)
        for j in range(cols // wide):
            span = slice(j * wide, (j + 1) * wide)
            scale = jnp.concatenate(
                [jnp.full((1, BLK), mask[tile_row + step // 8, tile_col + t].astype(jnp.float32)
                          * (1.0 / math.sqrt(W * F)), jnp.float32)
                 for t in range(j * wide // BLK, (j + 1) * wide // BLK)], axis=1)
            even, odd = [], []
            for h in range(2):
                at = step * 2 + h
                even.append(jnp.dot(even_mat[...], cross[0, at, :, :, span].reshape(F * 8, wide),
                                    preferred_element_type=jnp.float32))
                odd.append(jnp.dot(odd_mat[...], cross[1, at, :, :, span].reshape(F * 8, wide),
                                   preferred_element_type=jnp.float32))
            for m in range(HALF + 1):
                e = [v[m * 8:m * 8 + 8] for v in even]
                o = [v[m * 8:m * 8 + 8] for v in odd]
                if m < HALF:
                    buf[HALF + m, here, span] = (
                        jnp.concatenate([a + b for a, b in zip(e, o)], 0) * scale).astype(out.dtype)
                if m > 0:
                    buf[HALF - m, here, span] = (
                        jnp.concatenate([a - b for a, b in zip(e, o)], 0) * scale).astype(out.dtype)
        copy(step).start()
        return carry

    lax.fori_loop(0, rows // 16, one, 0, unroll=4)

    def finish(step, carry):
        copy(step).wait()
        return carry

    lax.fori_loop(0, rows // 16, finish, 0)


def lag_transform(cross, tile_mask):
    rows, cols = 256, 512
    even_mat, odd_mat = lag_matrices()
    vmem = pl.BlockSpec(memory_space=pltpu.VMEM)
    return pl.pallas_call(
        lag_kernel,
        in_specs=[pl.BlockSpec(memory_space=pltpu.SMEM), vmem, vmem, vmem],
        out_specs=pl.BlockSpec(memory_space=pl.ANY),
        out_shape=jax.ShapeDtypeStruct((LAGS, rows, cols), jnp.bfloat16),
        scratch_shapes=[pltpu.VMEM((LAGS, rows, cols), jnp.bfloat16), pltpu.SemaphoreType.DMA((rows // 16,))],
        compiler_params=pltpu.CompilerParams(vmem_limit_bytes=30 << 20),
        name="lag_transform",
    )(tile_mask, cross, even_mat, odd_mat)


def per_device(spectra, quality, tile_mask):
    cross = gather_cross(spectra, quality)
    return lag_transform(cross, tile_mask)


def solution(mesh):
    placed = (P(None, ("row", "col"), None), P(("row", "col")), P())
    return jax.shard_map(
        per_device, mesh=mesh, in_specs=placed, out_specs=P(None, "row", "col"), check_vma=False
    )
```

time: 127 us -> 123 us (0.969)
  Pallas kernels: 125 us -> 121 us
    pallas_call x1, Pallas kernels: 9.31 us -> 7.34 us  [lag_transform(): pl.pallas_call(lag_kernel, in_specs=[pl.BlockSpec(memory_space=pltpu.SMEM...]
    pallas_call x1, Pallas kernels: 115 us -> 114 us  [gather_cross(): pl.pallas_call(gather_kernel, out_shape=pltpu.VMEM((2, 32, F // 2, 16, 51...]
where the time goes in v4:
time: 123 us; the launch traced here: 121 us
  Pallas kernels  121 us (98%)
    pallas_call x1, Pallas kernels, gather_cross(): pl.pallas_call(gather_kernel, out_shape=pltpu.VMEM((2, 32, F // 2, 16, 51...  114 us
    pallas_call x1, Pallas kernels, lag_transform(): pl.pallas_call(lag_kernel, in_specs=[pl.BlockSpec(memory_space=pltpu.SMEM...  7.34 us

profile of v4, /device:TPU:27, one launch (start us, length us, event | category | flops | bytes accessed | tf_op | source)
XLA Modules:
  0.0 121.2 jit_solution(17315018187465555883)
XLA Ops:
  0.0 0.0 copy-start
  0.0 0.0 copy-start.1
  0.0 0.0 copy-start.2
  0.0 113.8 %gather_cross.1.cross = bf16[2,32,16,16,512]{4,3,2,1,0:T(8,128)(2,1)S(1)} custom-call(bf16[32,32,512]{2,1,0:T(8,128)(2,1)} %spectra.1, s32[1,32]{1,0:T(1,128)} %bitcast.1), custom_call_target="tpu_custom_call" | custom-call | tf_op jit(solution)/shard_map/gather_cross/pallas_call | solution.py:455
  113.8 0.0 copy-done
  113.8 0.0 copy-done.1
  113.9 0.0 copy-done.2
  113.9 7.3 %lag_transform.1 = bf16[64,256,512]{2,1,0:T(8,128)(2,1)} custom-call(s32[32,32]{1,0:T(8,128)S(1)} %copy-done.2, bf16[2,32,16,16,512]{4,3,2,1,0:T(8,128)(2,1)S(1)} %gather_cross.1.cross, bf16[264,256]{1,0:T(8,128)(2,1)S(1)} %copy-done.1, bf16[264,256]{1,0:T(8,128)(2,1)S(1)} %copy-done), custom_call_target="tpu_custom_call" | custom-call | tf_op jit(solution)/shard_map/lag_transform/pallas_call | solution.py:536
Async XLA Ops:
  0.0 113.8 %copy-start = (bf16[264,256]{1,0:T(8,128)(2,1)S(1)}, bf16[264,256]{1,0:T(8,128)(2,1)}, u32[]{:S(2)}) copy-start(bf16[264,256]{1,0:T(8,128)(2,1)} %constant.5.clone.odd_mat) | copy-start | bytes 405508
  0.0 113.8 %copy-start.1 = (bf16[264,256]{1,0:T(8,128)(2,1)S(1)}, bf16[264,256]{1,0:T(8,128)(2,1)}, u32[]{:S(2)}) copy-start(bf16[264,256]{1,0:T(8,128)(2,1)} %constant.4.clone.even_mat) | copy-start | bytes 405508
  0.0 113.9 %copy-start.2 = (s32[32,32]{1,0:T(8,128)S(1)}, s32[32,32]{1,0:T(8,128)}, u32[]{:S(2)}) copy-start(s32[32,32]{1,0:T(8,128)} %mask.1) | copy-start | bytes 12292

commit v5 on v4

--- a/solution.py
+++ b/solution.py
@@ -252,11 +252,6 @@
         rowb[ids['E0'], f] = values
 
     whiten(spectra, quality, put)
-    for i in range(len(ORDER[0])):
-        word = jnp.int32(ORDER[0][i])
-        for p in range(1, 8):
-            word = jnp.where(place == p, ORDER[p][i], word)
-        steps[i] = word
     pl.semaphore_wait(barrier, 8)
 
     def root_step(piece, g):
@@ -278,6 +273,11 @@
         return carry
 
     lax.fori_loop(0, NC, first, 0)
+    for i in range(len(ORDER[0])):
+        word = jnp.int32(ORDER[0][i])
+        for p in range(1, 8):
+            word = jnp.where(place == p, ORDER[p][i], word)
+        steps[i] = word
 
     def y_own(g):
         row_send(6, 'E0', g, partner)

time: 123 us -> 123 us (level)
  no operation moved by 1% of the time
where the time goes in v5:
time: 123 us; the launch traced here: 121 us
  Pallas kernels  121 us (98%)
    pallas_call x1, Pallas kernels, gather_cross(): pl.pallas_call(gather_kernel, out_shape=pltpu.VMEM((2, 32, F // 2, 16, 51...  114 us
    pallas_call x1, Pallas kernels, lag_transform(): pl.pallas_call(lag_kernel, in_specs=[pl.BlockSpec(memory_space=pltpu.SMEM...  7.34 us

profile of v5, /device:TPU:27, one launch (start us, length us, event | category | flops | bytes accessed | tf_op | source)
XLA Modules:
  0.0 121.2 jit_solution(14103234282809465196)
XLA Ops:
  0.0 0.0 copy-start
  0.0 0.0 copy-start.1
  0.0 0.0 copy-start.2
  0.0 113.8 %gather_cross.1.cross = bf16[2,32,16,16,512]{4,3,2,1,0:T(8,128)(2,1)S(1)} custom-call(bf16[32,32,512]{2,1,0:T(8,128)(2,1)} %spectra.1, s32[1,32]{1,0:T(1,128)} %bitcast.1), custom_call_target="tpu_custom_call" | custom-call | tf_op jit(solution)/shard_map/gather_cross/pallas_call | solution.py:455
  113.8 0.0 copy-done
  113.8 0.0 copy-done.1
  113.9 0.0 copy-done.2
  113.9 7.3 %lag_transform.1 = bf16[64,256,512]{2,1,0:T(8,128)(2,1)} custom-call(s32[32,32]{1,0:T(8,128)S(1)} %copy-done.2, bf16[2,32,16,16,512]{4,3,2,1,0:T(8,128)(2,1)S(1)} %gather_cross.1.cross, bf16[264,256]{1,0:T(8,128)(2,1)S(1)} %copy-done.1, bf16[264,256]{1,0:T(8,128)(2,1)S(1)} %copy-done), custom_call_target="tpu_custom_call" | custom-call | tf_op jit(solution)/shard_map/lag_transform/pallas_call | solution.py:536
Async XLA Ops:
  0.0 113.8 %copy-start = (bf16[264,256]{1,0:T(8,128)(2,1)S(1)}, bf16[264,256]{1,0:T(8,128)(2,1)}, u32[]{:S(2)}) copy-start(bf16[264,256]{1,0:T(8,128)(2,1)} %constant.5.clone.odd_mat) | copy-start | bytes 405508
  0.0 113.8 %copy-start.1 = (bf16[264,256]{1,0:T(8,128)(2,1)S(1)}, bf16[264,256]{1,0:T(8,128)(2,1)}, u32[]{:S(2)}) copy-start(bf16[264,256]{1,0:T(8,128)(2,1)} %constant.4.clone.even_mat) | copy-start | bytes 405508
  0.0 113.9 %copy-start.2 = (s32[32,32]{1,0:T(8,128)S(1)}, s32[32,32]{1,0:T(8,128)}, u32[]{:S(2)}) copy-start(s32[32,32]{1,0:T(8,128)} %mask.1) | copy-start | bytes 12292
